TPU v7x, 256 devices: a whole 4x4x8 slice. The times are simulated.
256 devices in a mesh: seq: 64 (over z, y, core), head: 4 (over x).
Axes of the slice: x: 4, y: 4, z: 8, core: 2. Of those that a mesh axis runs over, the one named last changes fastest.
Arguments:
- hidden_in: bfloat16 [16384, 2304], P(('seq', 'head')), may hold values from -6 to 6
- qkv_weight: bfloat16 [2304, 3, 2048], P(None, None, 'head'), may hold values from -0.125 to 0.125
- conv_weight: bfloat16 [3, 4, 2048], P(None, None, 'head'), may hold values from -3 to 3
- decay_log: float32 [16], P('head'), may hold values from -9 to -3
- dt_bias: float32 [2048], P('head'), may hold values from -3 to 3
- decay_down: bfloat16 [2304, 128], replicated, may hold values from -0.125 to 0.125
- decay_up: bfloat16 [128, 2048], P(None, 'head'), may hold values from -0.5 to 0.5
- beta_weight: bfloat16 [2304, 16], P(None, 'head'), may hold values from -0.125 to 0.125
- gate_down: bfloat16 [2304, 128], replicated, may hold values from -0.125 to 0.125
- gate_up: bfloat16 [128, 2048], P(None, 'head'), may hold values from -0.5 to 0.5
- norm_gain: float32 [128], replicated, may hold values from 0.1 to 1.9
- out_weight: bfloat16 [2048, 2304], P('head'), may hold values from -0.125 to 0.125
Outputs:
- layer_out: bfloat16 [16384, 2304], P(('seq', 'head'))
All inputs are finite; a program needn't handle non-finite values.
Results may differ from a plain program's by a relative error of at most 0.015.
Values may be sent and summed in bfloat16 or wider, within the bound.
A program may use at most 128 MiB of HBM per device.

v0:
```python
import math

import jax
import jax.numpy as jnp
from jax import lax
from jax.sharding import Mesh
from jax.sharding import PartitionSpec as P

SEQ = ("seq_0", "seq_1", "seq_2")
SEQ_HEAD = ("seq_0", "seq_1", "seq_2", "head")


exact_precision = lax.Precision.HIGHEST


def passed_along(block, axis, distance):
    devices = range(lax.axis_size(axis))
    route = [(i - distance, i) for i in devices if i - distance in devices]
    return lax.ppermute(block, axis, route)


def nothing_yet(value, identity):
    return jax.tree.map(
        lambda part, zero: jnp.zeros_like(part) + jnp.asarray(zero, part.dtype), value, identity
    )


def carried_in(value, axes, combine, identity):
    before = start = nothing_yet(value, identity)
    so_far = value
    for axis in reversed(axes):
        devices, here = (lax.axis_size(axis), lax.axis_index(axis))
        pieces = jax.tree.map(
            lambda part, kind: lax.all_gather(part.astype(kind), axis),
            so_far,
            jax.tree.map(lambda a: jnp.bfloat16 if a.dtype == jnp.float32 else a.dtype, value),
        )
        inside, so_far = (start, start)
        for k in range(devices):
            passed = k < here
            so_far = combine(
                so_far, jax.tree.map(lambda part, own: part[k].astype(own.dtype), pieces, value)
            )
            inside = jax.tree.map(lambda new, old: jnp.where(passed, new, old), so_far, inside)
        before = combine(inside, before)
    return before


def l2_normalize(values):
    return values * lax.rsqrt(jnp.sum(values * values, axis=-1, keepdims=True) + 1e-06)


def product(left, right):
    return jnp.einsum("hij,hjk->hik", left, right, precision=exact_precision)


def compose(earlier, later):
    first_map, first_shift = earlier
    second_map, second_shift = later
    return (product(second_map, first_map), product(second_map, first_shift) + second_shift)


def compose_single(earlier, later):
    first_map, first_shift = earlier
    second_map, second_shift = later
    return (
        jnp.dot(second_map, first_map, precision=exact_precision),
        jnp.dot(second_map, first_shift, precision=exact_precision) + second_shift,
    )


def block_terms(queries, key_rows, value_rows, log_decay, strength):
    row_count = key_rows.shape[1]
    head_size = key_rows.shape[2]
    cumulative = jnp.cumsum(log_decay, axis=1)
    middle = cumulative[:, row_count // 2 : row_count // 2 + 1]
    block_end = cumulative[:, row_count - 1 :]
    key_rise = key_rows * jnp.exp(cumulative - middle)
    key_fall = key_rows * jnp.exp(middle - cumulative)
    query_rise = queries * jnp.exp(cumulative - middle)
    positions = jnp.arange(row_count)
    strict_lower = positions[:, None] > positions[None, :]
    inclusive = positions[:, None] >= positions[None, :]
    key_mixing = jnp.where(
        strict_lower,
        jnp.einsum("htk,hjk->htj", key_rise, key_fall, precision=exact_precision)
        * strength[:, None, :],
        0.0,
    )
    attend = jnp.where(
        inclusive,
        jnp.einsum("htk,hjk->htj", query_rise, key_fall, precision=exact_precision)
        * strength[:, None, :],
        0.0,
    )
    nilpotent = -key_mixing
    inverse = jnp.eye(row_count, dtype=jnp.float32)[None] + nilpotent
    for _ in range(1, (row_count - 1).bit_length()):
        nilpotent = product(nilpotent, nilpotent)
        inverse = inverse + product(inverse, nilpotent)
    key_start = key_rows * jnp.exp(cumulative)
    query_start = queries * jnp.exp(cumulative)
    state_correction = product(inverse, value_rows)
    erasure = product(inverse, key_start)
    output_rows = product(attend, state_correction)
    raised_tensor = query_start - product(attend, erasure)
    key_stop_index = key_rows * jnp.exp(block_end - cumulative) * strength[:, :, None]
    eye_keys = jnp.eye(head_size, dtype=jnp.float32)
    transition = jnp.exp(block_end[:, 0])[:, :, None] * eye_keys[None] - jnp.einsum(
        "hjk,hjl->hkl", key_stop_index, erasure, precision=exact_precision
    )
    position_shift = jnp.einsum(
        "xpd,xpb->xdb", key_stop_index, state_correction, precision=exact_precision
    )
    return (output_rows, raised_tensor, transition, position_shift)


def recur(query_in, key_in, value_in, log_decay, strength, entry_state):
    row_count, head_count, head_size = key_in.shape
    queries = l2_normalize(query_in.astype(jnp.float32)) * head_size ** (-0.5)
    key_rows = l2_normalize(key_in.astype(jnp.float32))
    value_rows = value_in.astype(jnp.float32)
    block_len = math.gcd(row_count, 64)
    block_count = row_count // block_len

    def to_blocks(values):
        return values.reshape(block_count, block_len, head_count, -1).transpose(0, 2, 1, 3)

    strength_blocks = strength.reshape(block_count, block_len, head_count).transpose(0, 2, 1)
    eye_keys = jnp.eye(head_size, dtype=jnp.float32)
    neutral = (
        jnp.broadcast_to(eye_keys, (head_count, head_size, head_size)),
        jnp.zeros((head_count, head_size, head_size), jnp.float32),
    )

    def advance(carry, inputs):
        so_far_map, so_far_shift = carry
        output_rows, raised_tensor, transition, position_shift = block_terms(*inputs)
        output_rows = output_rows + product(raised_tensor, so_far_shift)
        raised_tensor = product(raised_tensor, so_far_map)
        return (compose(carry, (transition, position_shift)), (output_rows, raised_tensor))

    whole_pair, stacked = lax.scan(
        advance,
        neutral,
        (
            to_blocks(queries),
            to_blocks(key_rows),
            to_blocks(value_rows),
            to_blocks(log_decay),
            strength_blocks,
        ),
    )
    output_rows, raised_tensor = stacked
    incoming_state = entry_state(whole_pair)
    output_rows = output_rows + jnp.einsum(
        "owfp,wpc->owfc", raised_tensor, incoming_state, precision=exact_precision
    )
    return output_rows.transpose(0, 2, 1, 3).reshape(row_count, head_count, -1)


def shards(
    hidden_in,
    qkv_weight,
    conv_weight,
    decay_log,
    dt_bias,
    decay_down,
    decay_up,
    beta_weight,
    gate_down,
    gate_up,
    norm_gain,
    out_weight,
):
    gathered = lax.all_gather(hidden_in, "head", axis=0, tiled=True)
    row_count = gathered.shape[0]
    head_count = decay_log.shape[0]
    head_size = norm_gain.shape[0]
    full_width = head_count * head_size
    tap_count = conv_weight.shape[1]
    projected = jnp.dot(
        gathered,
        qkv_weight.reshape(qkv_weight.shape[0], 3 * full_width),
        preferred_element_type=jnp.float32,
    ).astype(jnp.bfloat16)
    projected = projected.reshape(row_count, 3, full_width)
    rim_rows = passed_along(projected[row_count - (tap_count - 1) :], SEQ, 1)
    padded = jnp.concatenate([rim_rows, projected], axis=0).astype(jnp.float32)
    taps = conv_weight.astype(jnp.float32)
    convolved = jnp.zeros((row_count, 3, full_width), jnp.float32)
    for tap_index in range(tap_count):
        convolved = convolved + padded[tap_index : tap_index + row_count] * taps[:, tap_index][None]
    convolved = jax.nn.silu(convolved).astype(jnp.bfloat16)
    query_in = convolved[:, 0].reshape(row_count, head_count, head_size)
    key_in = convolved[:, 1].reshape(row_count, head_count, head_size)
    value_in = convolved[:, 2].reshape(row_count, head_count, head_size)
    decay_low = jnp.dot(gathered, decay_down, preferred_element_type=jnp.float32).astype(
        jnp.bfloat16
    )
    raw_decay = jnp.dot(decay_low, decay_up, preferred_element_type=jnp.float32) + dt_bias
    log_decay = -jnp.exp(decay_log)[None, :, None] * jax.nn.softplus(raw_decay).reshape(
        row_count, head_count, head_size
    )
    strength = jax.nn.sigmoid(jnp.dot(gathered, beta_weight, preferred_element_type=jnp.float32))
    gate_low = jnp.dot(gathered, gate_down, preferred_element_type=jnp.float32).astype(jnp.bfloat16)
    out_gate = jax.nn.sigmoid(
        jnp.dot(gate_low, gate_up, preferred_element_type=jnp.float32)
    ).reshape(row_count, head_count, head_size)
    eye_single = jnp.eye(head_size, dtype=jnp.float32)
    zero_single = jnp.zeros((head_size, head_size), jnp.float32)

    def block_single(single_pair):
        return carried_in(single_pair, SEQ, compose_single, (eye_single, zero_single))[1]

    def block_entry(transfer_pair):
        return lax.map(block_single, transfer_pair)

    attended = recur(query_in, key_in, value_in, log_decay, strength, block_entry)
    inverse_rms = lax.rsqrt(jnp.mean(attended * attended, axis=-1, keepdims=True) + 1e-05)
    normed = (
        (attended * inverse_rms * norm_gain * out_gate)
        .astype(jnp.bfloat16)
        .reshape(row_count, full_width)
    )
    own_rows = lax.all_to_all(normed, "head", split_axis=0, concat_axis=1, tiled=True)
    summed = jnp.dot(
        own_rows,
        lax.all_gather(out_weight, "head", axis=0, tiled=True),
        preferred_element_type=jnp.float32,
    )
    return summed.astype(jnp.bfloat16)


def solution(mesh):
    finer = Mesh(
        mesh.devices.reshape(8, 4, 2, mesh.shape["head"]), ("seq_0", "seq_1", "seq_2", "head")
    )
    return jax.shard_map(
        shards,
        mesh=finer,
        in_specs=(
            P(SEQ_HEAD, None),
            P(None, None, "head"),
            P(None, None, "head"),
            P("head"),
            P("head"),
            P(),
            P(None, "head"),
            P(None, "head"),
            P(),
            P(None, "head"),
            P(),
            P("head", None),
        ),
        out_specs=P(SEQ_HEAD, None),
        check_vma=False,
    )
```

profile of v0, /device:TPU:192, one launch (start us, length us, event | category | flops | bytes accessed | tf_op | source)
XLA Modules:
  0.0 465.2 jit_solution(715077736735014275)
XLA Ops:
  8.1 10.3 %copy.38 = bf16[2304,3,512]{0,2,1:T(8,128)(2,1)} copy(bf16[2304,3,512]{2,0,1:T(8,128)(2,1)} %param.17) | data formatting | bytes 14155776 | tf_op args[1]
  18.5 18.3 %all-gather.19.cloned.1.call-done = bf16[256,2304]{1,0:T(8,128)(2,1)} async-done(((bf16[64,2304]{1,0:T(8,128)(2,1)}), bf16[256,2304]{1,0:T(8,128)(2,1)}) %all-gather.19.cloned.1.call-update) | async-done | bytes 1179664 | tf_op jit(solution)/shard_map/all_gather | solution.py:176
  36.9 5.5 %convolution_convert_fusion.1 = bf16[256,1536]{1,0:T(8,128)(2,1)S(1)} fusion(bf16[256,2304]{1,0:T(8,128)(2,1)} %all-gather.19.cloned.1.call-done, bf16[2304,1536]{0,1:T(8,128)(2,1)} %bitcast.359), kind=kOutput, calls=%fused_computation.146 | convolution fusion | flops 1812332544 | bytes 9043968 | tf_op jit(solution)/shard_map/dot_general | solution.py:182
  43.4 2.0 collective-permute-start
  45.4 1.6 compare_select_fusion
  47.1 1.2 reshape.144
  48.7 1.0 fusion.111
  50.1 4.9 %collective-permute-done = bf16[3,3,512]{0,2,1:T(8,128)(2,1)} collective-permute-done((bf16[3,3,512]{0,2,1:T(8,128)(2,1)}, bf16[3,3,512]{0,2,1:T(8,128)(2,1)}, u32[]{:S(2)}, u32[]{:S(2)}) %collective-permute-start) | collective-permute-done | bytes 9248 | tf_op jit(solution)/shard_map/ppermute | solution.py:19
  55.0 1.5 maximum_convert_fusion
  56.5 2.4 multiply_convert_fusion
  61.2 1.2 copy.41
  64.3 39.7 %while.30 = (s32[]{:T(128)}, f32[4,128,128]{2,1,0:T(8,128)S(1)}, f32[4,128,128]{2,1,0:T(8,128)S(1)}, f32[4,4,64,128]{3,2,0,1:T(8,128)}, f32[4,4,64,128]{3,2,0,1:...) while((s32[]{:T(128)}, f32[4,128,128]{2,1,0:T(8,128)S(1)}, ...), condition=%wide.region_4.5_spmd.clone, body=%wide.region_2.4_spmd.clone.sunk | while | flops 682688512 | bytes 10499228 | solution.py:143
  72.8 1.0 fusion.422
  79.8 1.0 fusion.421
  82.7 1.0 fusion.422
  89.8 1.0 fusion.421
  92.6 1.0 fusion.422
  99.7 1.0 fusion.421
  102.5 1.0 fusion.422
  104.1 333.6 %while.29 = (s32[]{:T(128)}, f32[4,128,128]{2,1,0:T(8,128)}, bf16[4,128,128]{2,1,0:T(8,128)(2,1)S(1)}, bf16[4,128,128]{2,1,0:T(8,128)(2,1)S(1)}, s32[]{:T(128)},...) while((s32[]{:T(128)}, f32[4,128,128]{2,1,0:T(8,128)}, ...), condition=%wide.region_6.7_spmd.clone.clone, body=%wide.region_5.6_spmd.clone.clone.sunk | while | flops 630226944 | bytes 6751127 | solution.py:217
  104.3 2.0 all_gather.54
  106.3 1.8 all_gather.55
  108.5 12.0 %all-gather.13 = bf16[512,128]{1,0:T(8,128)(2,1)S(1)} all-gather(bf16[128,128]{1,0:T(8,128)(2,1)S(1)} %get-tuple-element.334), channel_id=4, replica_groups=mesh['seq_0'=8,'seq_1'=4,'seq_2'=2,'head'=4] {'seq_1'}, dimensions={0}, use_global_device_ids=true | all-gather | bytes 163840 | tf_op jit(solution)/shard_map/while/body/eval_jaxpr/all_gather | solution.py:34
  120.8 12.0 %all-gather.12 = bf16[512,128]{1,0:T(8,128)(2,1)S(1)} all-gather(bf16[128,128]{1,0:T(8,128)(2,1)S(1)} %get-tuple-element.332), channel_id=2, replica_groups=mesh['seq_0'=8,'seq_1'=4,'seq_2'=2,'head'=4] {'seq_1'}, dimensions={0}, use_global_device_ids=true | all-gather | bytes 163840 | tf_op jit(solution)/shard_map/while/body/eval_jaxpr/all_gather | solution.py:34
  134.2 25.6 %all-gather.14 = bf16[1024,128]{1,0:T(8,128)(2,1)S(1)} all-gather(bf16[128,128]{1,0:T(8,128)(2,1)S(1)} %get-tuple-element.335), channel_id=5, replica_groups=mesh['seq_0'=8,'seq_1'=4,'seq_2'=2,'head'=4] {'seq_0'}, dimensions={0}, use_global_device_ids=true | all-gather | bytes 294912 | tf_op jit(solution)/shard_map/while/body/eval_jaxpr/all_gather | solution.py:34
  160.6 24.8 %all-gather.15 = bf16[1024,128]{1,0:T(8,128)(2,1)S(1)} all-gather(bf16[128,128]{1,0:T(8,128)(2,1)S(1)} %get-tuple-element.336), channel_id=3, replica_groups=mesh['seq_0'=8,'seq_1'=4,'seq_2'=2,'head'=4] {'seq_0'}, dimensions={0}, use_global_device_ids=true | all-gather | bytes 294912 | tf_op jit(solution)/shard_map/while/body/eval_jaxpr/all_gather | solution.py:34
  188.2 1.8 all_gather.54
  190.1 1.8 all_gather.55
  192.3 12.0 %all-gather.13 = bf16[512,128]{1,0:T(8,128)(2,1)S(1)} all-gather(bf16[128,128]{1,0:T(8,128)(2,1)S(1)} %get-tuple-element.334), channel_id=4, replica_groups=mesh['seq_0'=8,'seq_1'=4,'seq_2'=2,'head'=4] {'seq_1'}, dimensions={0}, use_global_device_ids=true | all-gather | bytes 163840 | tf_op jit(solution)/shard_map/while/body/eval_jaxpr/all_gather | solution.py:34
  204.6 12.0 %all-gather.12 = bf16[512,128]{1,0:T(8,128)(2,1)S(1)} all-gather(bf16[128,128]{1,0:T(8,128)(2,1)S(1)} %get-tuple-element.332), channel_id=2, replica_groups=mesh['seq_0'=8,'seq_1'=4,'seq_2'=2,'head'=4] {'seq_1'}, dimensions={0}, use_global_device_ids=true | all-gather | bytes 163840 | tf_op jit(solution)/shard_map/while/body/eval_jaxpr/all_gather | solution.py:34
  218.0 25.0 %all-gather.14 = bf16[1024,128]{1,0:T(8,128)(2,1)S(1)} all-gather(bf16[128,128]{1,0:T(8,128)(2,1)S(1)} %get-tuple-element.335), channel_id=5, replica_groups=mesh['seq_0'=8,'seq_1'=4,'seq_2'=2,'head'=4] {'seq_0'}, dimensions={0}, use_global_device_ids=true | all-gather | bytes 294912 | tf_op jit(solution)/shard_map/while/body/eval_jaxpr/all_gather | solution.py:34
  243.7 24.8 %all-gather.15 = bf16[1024,128]{1,0:T(8,128)(2,1)S(1)} all-gather(bf16[128,128]{1,0:T(8,128)(2,1)S(1)} %get-tuple-element.336), channel_id=3, replica_groups=mesh['seq_0'=8,'seq_1'=4,'seq_2'=2,'head'=4] {'seq_0'}, dimensions={0}, use_global_device_ids=true | all-gather | bytes 294912 | tf_op jit(solution)/shard_map/while/body/eval_jaxpr/all_gather | solution.py:34
  271.4 1.8 all_gather.54
  273.2 1.8 all_gather.55
  275.4 12.0 %all-gather.13 = bf16[512,128]{1,0:T(8,128)(2,1)S(1)} all-gather(bf16[128,128]{1,0:T(8,128)(2,1)S(1)} %get-tuple-element.334), channel_id=4, replica_groups=mesh['seq_0'=8,'seq_1'=4,'seq_2'=2,'head'=4] {'seq_1'}, dimensions={0}, use_global_device_ids=true | all-gather | bytes 163840 | tf_op jit(solution)/shard_map/while/body/eval_jaxpr/all_gather | solution.py:34
  287.8 12.0 %all-gather.12 = bf16[512,128]{1,0:T(8,128)(2,1)S(1)} all-gather(bf16[128,128]{1,0:T(8,128)(2,1)S(1)} %get-tuple-element.332), channel_id=2, replica_groups=mesh['seq_0'=8,'seq_1'=4,'seq_2'=2,'head'=4] {'seq_1'}, dimensions={0}, use_global_device_ids=true | all-gather | bytes 163840 | tf_op jit(solution)/shard_map/while/body/eval_jaxpr/all_gather | solution.py:34
  301.1 25.0 %all-gather.14 = bf16[1024,128]{1,0:T(8,128)(2,1)S(1)} all-gather(bf16[128,128]{1,0:T(8,128)(2,1)S(1)} %get-tuple-element.335), channel_id=5, replica_groups=mesh['seq_0'=8,'seq_1'=4,'seq_2'=2,'head'=4] {'seq_0'}, dimensions={0}, use_global_device_ids=true | all-gather | bytes 294912 | tf_op jit(solution)/shard_map/while/body/eval_jaxpr/all_gather | solution.py:34
  326.9 24.8 %all-gather.15 = bf16[1024,128]{1,0:T(8,128)(2,1)S(1)} all-gather(bf16[128,128]{1,0:T(8,128)(2,1)S(1)} %get-tuple-element.336), channel_id=3, replica_groups=mesh['seq_0'=8,'seq_1'=4,'seq_2'=2,'head'=4] {'seq_0'}, dimensions={0}, use_global_device_ids=true | all-gather | bytes 294912 | tf_op jit(solution)/shard_map/while/body/eval_jaxpr/all_gather | solution.py:34
  354.5 1.8 all_gather.54
  356.4 1.8 all_gather.55
  358.6 12.0 %all-gather.13 = bf16[512,128]{1,0:T(8,128)(2,1)S(1)} all-gather(bf16[128,128]{1,0:T(8,128)(2,1)S(1)} %get-tuple-element.334), channel_id=4, replica_groups=mesh['seq_0'=8,'seq_1'=4,'seq_2'=2,'head'=4] {'seq_1'}, dimensions={0}, use_global_device_ids=true | all-gather | bytes 163840 | tf_op jit(solution)/shard_map/while/body/eval_jaxpr/all_gather | solution.py:34
  370.9 12.0 %all-gather.12 = bf16[512,128]{1,0:T(8,128)(2,1)S(1)} all-gather(bf16[128,128]{1,0:T(8,128)(2,1)S(1)} %get-tuple-element.332), channel_id=2, replica_groups=mesh['seq_0'=8,'seq_1'=4,'seq_2'=2,'head'=4] {'seq_1'}, dimensions={0}, use_global_device_ids=true | all-gather | bytes 163840 | tf_op jit(solution)/shard_map/while/body/eval_jaxpr/all_gather | solution.py:34
  384.3 25.0 %all-gather.14 = bf16[1024,128]{1,0:T(8,128)(2,1)S(1)} all-gather(bf16[128,128]{1,0:T(8,128)(2,1)S(1)} %get-tuple-element.335), channel_id=5, replica_groups=mesh['seq_0'=8,'seq_1'=4,'seq_2'=2,'head'=4] {'seq_0'}, dimensions={0}, use_global_device_ids=true | all-gather | bytes 294912 | tf_op jit(solution)/shard_map/while/body/eval_jaxpr/all_gather | solution.py:34
  410.0 24.8 %all-gather.15 = bf16[1024,128]{1,0:T(8,128)(2,1)S(1)} all-gather(bf16[128,128]{1,0:T(8,128)(2,1)S(1)} %get-tuple-element.336), channel_id=3, replica_groups=mesh['seq_0'=8,'seq_1'=4,'seq_2'=2,'head'=4] {'seq_0'}, dimensions={0}, use_global_device_ids=true | all-gather | bytes 294912 | tf_op jit(solution)/shard_map/while/body/eval_jaxpr/all_gather | solution.py:34
  437.7 1.8 multiply_reduce_fusion
  440.3 1.7 fusion.106
  442.0 10.2 %all_to_all.19 = bf16[4,64,512]{2,1,0:T(8,128)(2,1)S(1)} all-to-all(bf16[4,64,512]{2,1,0:T(8,128)(2,1)S(1)} %bitcast.376), channel_id=1, replica_groups=mesh['seq_0'=8,'seq_1'=4,'seq_2'=2,'head'=4] {'head'}, dimensions={0} | all-to-all | bytes 524288 | tf_op jit(solution)/shard_map/all_to_all | solution.py:226
  452.3 6.1 %convolution_convert_fusion = bf16[64,2304]{1,0:T(8,128)(2,1)} fusion(bf16[64,2048]{1,0:T(8,128)(2,1)S(1)} %bitcast.364, bf16[2048,2304]{1,0:T(8,128)(2,1)} %all-gather.21.cloned.1.call-done), kind=kOutput, calls=%fused_computation.145 | convolution fusion | flops 604127232 | bytes 9994240 | tf_op jit(solution)/shard_map/dot_general | solution.py:227
  (307 shorter events, 61.6 us)
Async XLA Ops:
  6.5 38.9 %copy-start = (bf16[2304,128]{1,0:T(8,128)(2,1)S(1)}, bf16[2304,128]{1,0:T(8,128)(2,1)}, u32[]{:S(2)}) copy-start(bf16[2304,128]{1,0:T(8,128)(2,1)} %param.21) | copy-start | bytes 1769476
  6.5 30.3 %all-gather.19.cloned.1.call-start = ((), (), s32[]{:S(2)}) async-start(), calls=%async_computation.1 | async-start | bytes 1474560 | tf_op jit(solution)/shard_map/all_gather | solution.py:176
  7.3 445.0 %all-gather.21.cloned.1.call-start = ((), (), s32[]{:S(2)}) async-start(), calls=%async_computation.2 | async-start | bytes 11796480 | tf_op jit(solution)/shard_map/all_gather | solution.py:229
  8.1 10.4 %copy-start.6 = (bf16[3,4,512]{2,1,0:T(4,128)(2,1)S(1)}, bf16[3,4,512]{2,1,0:T(4,128)(2,1)}, u32[]{:S(2)}) copy-start(bf16[3,4,512]{2,1,0:T(4,128)(2,1)} %param.18) | copy-start | bytes 36868
  8.1 10.4 %copy-start.12 = (f32[4]{0:T(128)S(1)}, f32[4]{0:T(128)}, u32[]{:S(2)}) copy-start(f32[4]{0:T(128)} %param.19) | copy-start | bytes 52
  8.1 10.4 %copy-start.8 = (f32[128]{0:T(128)S(1)}, f32[128]{0:T(128)}, u32[]{:S(2)}) copy-start(f32[128]{0:T(128)} %param.26) | copy-start | bytes 1540
  36.9 8.6 %copy-start.1 = (bf16[256,2304]{1,0:T(8,128)(2,1)S(1)}, bf16[256,2304]{1,0:T(8,128)(2,1)}, u32[]{:S(2)}) copy-start(bf16[256,2304]{1,0:T(8,128)(2,1)} %all-gather.19.cloned.1.call-done) | copy-start | bytes 3538948
  36.9 8.6 %copy-start.9 = (bf16[128,512]{1,0:T(8,128)(2,1)S(1)}, bf16[128,512]{1,0:T(8,128)(2,1)}, u32[]{:S(2)}) copy-start(bf16[128,512]{1,0:T(8,128)(2,1)} %param.22) | copy-start | bytes 393220
  36.9 8.6 %copy-start.11 = (f32[512]{0:T(512)S(1)}, f32[512]{0:T(512)}, u32[]{:S(2)}) copy-start(f32[512]{0:T(512)} %param.20) | copy-start | bytes 6148
  43.4 4.9 %copy-start.7 = (bf16[2304,4]{0,1:T(4,128)(2,1)S(1)}, bf16[2304,4]{0,1:T(4,128)(2,1)}, u32[]{:S(2)}) copy-start(bf16[2304,4]{0,1:T(4,128)(2,1)} %param.23) | copy-start | bytes 55300
  43.4 11.6 %collective-permute-start = (bf16[3,3,512]{0,2,1:T(8,128)(2,1)}, bf16[3,3,512]{0,2,1:T(8,128)(2,1)}, u32[]{:S(2)}, u32[]{:S(2)}) collective-permute-start(bf16[3,3,512]{0,2,1:T(8,128)(2,1)} %bitcast.2), channel_id=1, source_target_pairs={{0,4},{4,8},{8,12},{12,16},{16,20},{20,24},{24,28},{28,32},{32,36}... | collective-permute-start | bytes 27656 | tf_op jit(solution)/shard_map/ppermute | solution.py:19
  62.7 0.9 copy-start.5
  104.0 333.6 %copy-start.3 = (f32[4,4,64,128]{3,2,0,1:T(8,128)S(1)}, f32[4,4,64,128]{3,2,0,1:T(8,128)}, u32[]{:S(2)}) copy-start(f32[4,4,64,128]{3,2,0,1:T(8,128)} %get-tuple-element.102) | copy-start | bytes 1572868
  104.0 333.6 %copy-start.4 = (f32[4,4,64,128]{3,2,0,1:T(8,128)S(1)}, f32[4,4,64,128]{3,2,0,1:T(8,128)}, u32[]{:S(2)}) copy-start(f32[4,4,64,128]{3,2,0,1:T(8,128)} %get-tuple-element.106) | copy-start | bytes 1572868
  437.7 2.6 copy-start.2
  437.7 2.6 copy-start.10
Sparse Core Ops, SparseCore 0:
  9.1 27.6 all-gather.18
  38.7 95.0 all-gather.20
where the time goes:
time: 469 us; the launch traced here: 465 us
  blocking collectives  321 us (68%)
  matrix products  73 us (16%)
  waiting for transfers between devices  24.7 us (5%)
  local copies, waits for them, and re-layouts  21.3 us (5%)
  between operations  13.8 us (3%)
  other arithmetic  7.51 us (2%)
    all_gather x24, blocking collectives, carried_in(): lax.all_gather(part.astype(kind), axis)  311 us
    dot_general x72, matrix products, product(): return jnp.einsum('hij,hjk->hik', left, right, precision=exact_precision)  25.7 us
    all_gather x1, waiting for transfers between devices, shards(): gathered = lax.all_gather(hidden_in, 'head', axis=0, tiled=True)  18.3 us
    dot_general x68, matrix products, compose_single(): jnp.dot(second_map, first_shift, precision=exact_precision) + second_shift  15.2 us
    unnamed x29, local copies, waits for them, and re-layouts  10.7 us
    all_to_all x1, blocking collectives, shards(): lax.all_to_all(normed, 'head', split_axis=0, concat_axis=1, tiled=True)  10.2 us
  transfers between devices with their start and end apart: 3, of which 2 were waited for; matrix products, arithmetic and copies ran while one was open for 20% of the time, Pallas kernels for 0%

commit v1 on v0

v1 whole, which is shorter than its diff:
```python
import functools

import jax
import jax.numpy as jnp
import numpy as np
from jax import lax
from jax.experimental import pallas as pl
from jax.experimental.pallas import tpu as pltpu
from jax.sharding import PartitionSpec as P

F32 = jnp.float32
BF16 = jnp.bfloat16
MESH = pl.DeviceIdType.MESH

HALO = 16
EDGE = 8
HALF = 128
LEVELS = (1, 2, 4, 8, 16, 32, 64)
PLANE = 8


def span_matrix():
    r, i = np.arange(HALF)[:, None], np.arange(HALF)[None, :]
    rows = []
    for size in LEVELS:
        middle = (r // (2 * size)) * 2 * size + size - 1
        late = (r % (2 * size)) >= size
        rows.append(np.where(late, (i > middle) & (i <= r), (i > r) & (i <= middle)))
    rows.append(i <= r)
    rows.append(i > r)
    spans = np.concatenate(rows, axis=0)
    return np.concatenate([spans, spans], axis=1).astype(np.float32)


def mm(a, b, dims=((1,), (0,))):
    return lax.dot_general(
        a.astype(BF16), b.astype(BF16), (dims, ((), ())), preferred_element_type=F32
    )


def sigmoid(v):
    return 1.0 / (1.0 + jnp.exp(-v))


def gather_kernel(seq_size, x_ref, out_ref, zero_ref, send_sem, recv_sem, edge_sem, local_sem):
    s = lax.axis_index("seq")
    h = lax.axis_index("head")
    right, left = lax.rem(h + 1, 4), lax.rem(h + 3, 4)
    rows = x_ref.shape[0]
    half = rows // 2
    has_next = s < seq_size - 1
    sends_edge = jnp.logical_and(h == 3, has_next)

    barrier = pltpu.get_barrier_semaphore()
    pl.semaphore_signal(barrier, 1, device_id={"head": right}, device_id_type=MESH)
    pl.semaphore_signal(barrier, 1, device_id={"head": left}, device_id_type=MESH)

    @pl.when(s > 0)
    def _():
        pl.semaphore_signal(
            barrier, 1, device_id={"seq": s - 1, "head": 3}, device_id_type=MESH
        )

    zero_ref[...] = jnp.zeros_like(zero_ref)
    own = pltpu.make_async_copy(
        x_ref, out_ref.at[pl.ds(pl.multiple_of(HALO + h * rows, 16), rows)], local_sem.at[0]
    )
    own.start()
    blank = pltpu.make_async_copy(zero_ref.at[pl.ds(0, EDGE)], out_ref.at[pl.ds(0, EDGE)], local_sem.at[1])
    blank.start()
    blank_edge = pltpu.make_async_copy(
        zero_ref.at[pl.ds(EDGE, EDGE)], out_ref.at[pl.ds(EDGE, EDGE)], local_sem.at[2]
    )

    @pl.when(s == 0)
    def _():
        blank_edge.start()

    @pl.when(sends_edge)
    def _():
        pl.semaphore_wait(barrier, 6)

    @pl.when(jnp.logical_not(sends_edge))
    def _():
        pl.semaphore_wait(barrier, 2)

    def place(owner, part):
        return out_ref.at[pl.ds(pl.multiple_of(HALO + owner * rows + part * half, 16), half)]

    def piece(src, owner, part, target, k):
        return pltpu.make_async_remote_copy(
            src_ref=src,
            dst_ref=place(owner, part),
            send_sem=send_sem.at[k],
            recv_sem=recv_sem.at[k],
            device_id={"head": target},
            device_id_type=MESH,
        )

    mine = [x_ref.at[pl.ds(0, half)], x_ref.at[pl.ds(half, half)]]
    to_right = [piece(mine[0], h, 0, right, 0), piece(mine[1], h, 1, right, 1)]
    to_left = [piece(mine[1], h, 1, left, 2), piece(mine[0], h, 0, left, 3)]
    to_right[0].start()
    to_left[0].start()
    to_right[1].start()
    to_left[1].start()

    def edge(target):
        return pltpu.make_async_remote_copy(
            src_ref=x_ref.at[pl.ds(rows - EDGE, EDGE)],
            dst_ref=out_ref.at[pl.ds(EDGE, EDGE)],
            send_sem=edge_sem.at[target],
            recv_sem=edge_sem.at[4],
            device_id={"seq": s + 1, "head": target},
            device_id_type=MESH,
        )

    @pl.when(sends_edge)
    def _():
        for target in range(4):
            edge(target).start()

    far = lax.rem(h + 2, 4)
    pass_right = piece(place(left, 0), left, 0, right, 4)
    pass_left = piece(place(right, 1), right, 1, left, 5)
    piece(mine[0], left, 0, right, 0).wait_recv()
    pass_right.start()
    piece(mine[1], right, 1, left, 2).wait_recv()
    pass_left.start()
    piece(mine[1], left, 1, right, 1).wait_recv()
    piece(mine[0], right, 0, left, 3).wait_recv()
    piece(mine[0], far, 0, right, 4).wait_recv()
    piece(mine[1], far, 1, left, 5).wait_recv()

    @pl.when(s > 0)
    def _():
        edge(0).wait_recv()

    @pl.when(s == 0)
    def _():
        blank_edge.wait()

    for copy in (*to_right, *to_left, pass_right, pass_left):
        copy.wait_send()

    @pl.when(sends_edge)
    def _():
        for target in range(4):
            edge(target).wait_send()

    own.wait()
    blank.wait()


def gather(seq_size, x):
    rows, width = x.shape
    return pl.pallas_call(
        functools.partial(gather_kernel, seq_size),
        name="gather",
        out_shape=jax.ShapeDtypeStruct((HALO + 4 * rows, width), x.dtype),
        in_specs=[pl.BlockSpec(memory_space=pl.ANY)],
        out_specs=pl.BlockSpec(memory_space=pl.ANY),
        scratch_shapes=[
            pltpu.VMEM((HALO, width), x.dtype),
            pltpu.SemaphoreType.DMA((6,)),
            pltpu.SemaphoreType.DMA((6,)),
            pltpu.SemaphoreType.DMA((5,)),
            pltpu.SemaphoreType.DMA((3,)),
        ],
        compiler_params=pltpu.CompilerParams(collective_id=0, has_side_effects=True),
    )(x)


def block_kernel(
    xg_ref, w_ref, down_ref, gdown_ref, beta_ref, up_ref, gup_ref, conv_ref, dlog_ref, bias_ref,
    span_ref, o_ref, r_ref, gate_ref, z_ref, proj_ref, q_ref, k_ref, v_ref, e_ref,
):
    count = xg_ref.shape[0] - HALO
    width = w_ref.shape[2]
    heads = width // 128
    x = xg_ref[HALO:, :]

    low = jnp.dot(x, down_ref[...], preferred_element_type=F32).astype(BF16)
    raw = jnp.dot(low, up_ref[...], preferred_element_type=F32) + bias_ref[...]
    soft = jnp.maximum(raw, 0.0) + jnp.log1p(jnp.exp(-jnp.abs(raw)))
    rate = jnp.concatenate(
        [jnp.exp(jnp.full((1, 128), dlog_ref[i], F32)) for i in range(heads)], axis=1
    )
    log_decay = -rate * soft
    for c in range(2):
        part = log_decay[c * HALF : (c + 1) * HALF]
        top = part.astype(BF16)
        rest = (part - top.astype(F32)).astype(BF16)
        e_ref[c] = jnp.exp(
            jnp.dot(
                span_ref[...], jnp.concatenate([top, rest], axis=0), preferred_element_type=F32
            )
        )
    gate_low = jnp.dot(x, gdown_ref[...], preferred_element_type=F32).astype(BF16)
    gate_ref[...] = sigmoid(jnp.dot(gate_low, gup_ref[...], preferred_element_type=F32))
    beta = sigmoid(
        lax.dot_general(
            x, beta_ref[...], (((1,), (1,)), ((), ())), preferred_element_type=F32
        )
    )

    for c, target in enumerate((q_ref, k_ref, v_ref)):
        proj_ref[...] = (
            jnp.dot(xg_ref[...], w_ref[c], preferred_element_type=F32).astype(BF16).astype(F32)
        )
        taps = conv_ref[c].astype(F32)
        total = proj_ref[pl.ds(HALO - 3, count), :] * taps[0:1]
        for i in range(1, 4):
            total = total + proj_ref[pl.ds(HALO - 3 + i, count), :] * taps[i : i + 1]
        total = (total * sigmoid(total)).astype(BF16).astype(F32)
        if c == 2:
            target[...] = total
            continue
        for i in range(heads):
            lanes = slice(i * 128, (i + 1) * 128)
            u = total[:, lanes]
            scale = lax.rsqrt(jnp.sum(u * u, axis=1, keepdims=True) + 1e-06)
            if c == 0:
                scale = scale * (128**-0.5)
            target[:, lanes] = u * scale

    t = lax.broadcasted_iota(jnp.int32, (HALF, HALF), 0)
    j = lax.broadcasted_iota(jnp.int32, (HALF, HALF), 1)
    row = lax.broadcasted_iota(jnp.int32, (HALF, 128), 0)
    masks = [
        ((t ^ j) >= size) & ((t ^ j) < 2 * size) & (t > j) for size in LEVELS
    ]
    diagonal = t == j

    pairs = [(i, c) for i in range(heads) for c in range(2)]
    lanes_of = [slice(i * 128, (i + 1) * 128) for i in range(heads)]
    rows_of = [slice(c * HALF, (c + 1) * HALF) for c in range(2)]
    strength = {
        (i, c): jnp.broadcast_to(beta[rows_of[c], i : i + 1], (HALF, 128)) for i, c in pairs
    }
    attend, inverse = {}, {}
    for i, c in pairs:
        kc, qc = k_ref[rows_of[c], lanes_of[i]], q_ref[rows_of[c], lanes_of[i]]
        own = jnp.sum(qc * kc, axis=1, keepdims=True) * strength[i, c]
        attend[i, c] = jnp.where(diagonal, own, 0.0)
        inverse[i, c] = jnp.where(diagonal, 1.0, 0.0)
    for n, size in enumerate(LEVELS):
        for i, c in pairs:
            kc, qc = k_ref[rows_of[c], lanes_of[i]], q_ref[rows_of[c], lanes_of[i]]
            fade = e_ref[c, n * HALF : (n + 1) * HALF, lanes_of[i]]
            late = (row & size) != 0
            kx = (kc * fade * jnp.where(late, 1.0, strength[i, c])).astype(BF16)
            qx = (qc * fade).astype(BF16)
            both = mm(jnp.concatenate([kx, qx], axis=0), kx, ((1,), (1,)))
            mixing = jnp.where(masks[n], both[:HALF], 0.0)
            attend[i, c] = jnp.where(masks[n], both[HALF:], attend[i, c])
            if size == 1:
                inverse[i, c] = inverse[i, c] - mixing
            else:
                own = inverse[i, c].astype(BF16)
                inverse[i, c] = inverse[i, c] - mm(mm(own, mixing), own)

    n = len(LEVELS)
    for i in range(heads):
        lanes = lanes_of[i]
        rise = [e_ref[c, n * HALF : (n + 1) * HALF, lanes] for c in range(2)]
        fall = [e_ref[c, (n + 1) * HALF : (n + 2) * HALF, lanes] for c in range(2)]
        whole = [part[HALF - 1 : HALF] for part in rise]
        k = [k_ref[rows_of[c], lanes] for c in range(2)]
        q = [q_ref[rows_of[c], lanes] for c in range(2)]
        k_rise = [k[c] * rise[c] for c in range(2)]
        q_rise = [q[c] * rise[c] for c in range(2)]
        k_fall = [k[c] * fall[c] * strength[i, c] for c in range(2)]
        cross = mm(jnp.concatenate([k_rise[1], q_rise[1]], axis=0), k_fall[0], ((1,), (1,)))
        first = mm(
            inverse[i, 0], jnp.concatenate([v_ref[rows_of[0], lanes], k_rise[0]], axis=1)
        ).astype(BF16)
        second = jnp.concatenate([v_ref[rows_of[1], lanes], k_rise[1] * whole[0]], axis=1)
        second = mm(inverse[i, 1], second - mm(cross[:HALF], first)).astype(BF16)
        out = [mm(attend[i, 0], first), mm(cross[HALF:], first) + mm(attend[i, 1], second)]
        for c in range(2):
            o_ref[rows_of[c], lanes] = out[c][:, :128]
        r_ref[rows_of[0], lanes] = (q_rise[0] - out[0][:, 128:]).astype(BF16)
        r_ref[rows_of[1], lanes] = (q_rise[1] * whole[0] - out[1][:, 128:]).astype(BF16)
        stop = jnp.concatenate([k_fall[0] * whole[1], k_fall[1]], axis=0).astype(BF16)
        z = mm(jnp.concatenate([first, second], axis=0), stop, ((0,), (0,)))
        move = jnp.where(diagonal, whole[0] * whole[1], 0.0) - z[128:]
        z_ref[i, 0:64] = z[0:64].astype(BF16)
        z_ref[i, 64:192] = move.astype(BF16)
        z_ref[i, 192:256] = z[64:128].astype(BF16)


def block(xg, w, down, gdown, beta, up, gup, conv, dlog, bias, span):
    count = xg.shape[0] - HALO
    width = w.shape[2]
    heads = width // 128
    vmem = pl.BlockSpec(memory_space=pltpu.VMEM)
    smem = pl.BlockSpec(memory_space=pltpu.SMEM)
    return pl.pallas_call(
        block_kernel,
        name="block",
        out_shape=(
            jax.ShapeDtypeStruct((count, width), F32),
            jax.ShapeDtypeStruct((count, width), BF16),
            jax.ShapeDtypeStruct((count, width), F32),
            jax.ShapeDtypeStruct((heads, 256, 128), BF16),
        ),
        in_specs=[vmem] * 8 + [smem] + [vmem] * 2,
        out_specs=(vmem,) * 4,
        scratch_shapes=[
            pltpu.VMEM((HALO + count, width), F32),
            pltpu.VMEM((count, width), F32),
            pltpu.VMEM((count, width), F32),
            pltpu.VMEM((count, width), F32),
            pltpu.VMEM((2, (len(LEVELS) + 2) * HALF, width), F32),
        ],
        compiler_params=pltpu.CompilerParams(vmem_limit_bytes=56 << 20),
    )(xg, w, down, gdown, beta, up, gup, conv, dlog, bias, span)


def finish_kernel(
    depth, z_ref, o_ref, r_ref, gate_ref, gain_ref, w_ref, out_ref,
    zin, pre, total, zall, held, lead, state, normed, part, sums, inbox,
    a_send, a_recv, b_send, b_recv, c_send, c_recv, d_send, d_recv,
):
    s = lax.axis_index("seq")
    h = lax.axis_index("head")
    z = lax.div(s, PLANE)
    p = lax.rem(s, PLANE)
    y, core = lax.div(p, 2), lax.rem(p, 2)
    base = z * PLANE
    right, left = lax.rem(h + 1, 4), lax.rem(h + 3, 4)
    map_at = pl.multiple_of(64 * (1 - core), 64)
    shift_at = pl.multiple_of(128 * core, 128)

    barrier = pltpu.get_barrier_semaphore()
    for d in range(1, PLANE):
        pl.semaphore_signal(
            barrier, 1, device_id={"seq": base + lax.rem(p + d, PLANE)}, device_id_type=MESH
        )
    pl.semaphore_signal(barrier, 1, device_id={"head": right}, device_id_type=MESH)
    pl.semaphore_signal(barrier, 1, device_id={"head": left}, device_id_type=MESH)

    def greet(k, _):
        pl.semaphore_signal(barrier, 1, device_id={"seq": k * PLANE + p}, device_id_type=MESH)
        return 0

    lax.fori_loop(0, z, greet, 0)
    pl.semaphore_wait(barrier, PLANE - 1 + 2 + (depth - 1 - z))

    def to_owner(d):
        q = lax.rem(p + d, PLANE)
        here = pl.ds(pl.multiple_of(64 * lax.rem(q, 2), 64), 192)
        return pltpu.make_async_remote_copy(
            src_ref=z_ref.at[lax.div(q, 2), here],
            dst_ref=zin.at[p],
            send_sem=a_send.at[d],
            recv_sem=a_recv.at[p],
            device_id={"seq": base + q},
            device_id_type=MESH,
        )

    for d in range(1, PLANE):
        to_owner(d).start()
    zin[p] = z_ref[y, pl.ds(pl.multiple_of(64 * core, 64), 192), :]

    def arrived(k):
        @pl.when(p != k)
        def _():
            pltpu.make_async_remote_copy(
                src_ref=zin.at[k],
                dst_ref=zin.at[k],
                send_sem=a_send.at[0],
                recv_sem=a_recv.at[k],
                device_id={"seq": s},
                device_id_type=MESH,
            ).wait_recv()

    eye = lax.broadcasted_iota(jnp.int32, (128, 128), 0) == lax.broadcasted_iota(
        jnp.int32, (128, 128), 1
    )
    pre[0, 0:128] = jnp.where(eye, 1.0, 0.0).astype(BF16)
    pre[0, 128:192] = jnp.zeros((64, 128), BF16)
    arrived(0)
    move = zin[0, pl.ds(map_at, 128), :]
    shift = zin[0, pl.ds(shift_at, 64), :]
    so_far = jnp.concatenate([move, shift], axis=0)
    pre[1] = so_far
    for k in range(1, PLANE):
        arrived(k)
        move = zin[k, pl.ds(map_at, 128), :]
        shift = zin[k, pl.ds(shift_at, 64), :].astype(F32)
        nxt = mm(so_far, move)
        so_far = jnp.concatenate(
            [nxt[:128].astype(BF16), (nxt[128:] + shift).astype(BF16)], axis=0
        )
        if k < PLANE - 1:
            pre[k + 1] = so_far
        else:
            total[...] = so_far

    def to_later(k):
        return pltpu.make_async_remote_copy(
            src_ref=total,
            dst_ref=zall.at[z],
            send_sem=b_send.at[k],
            recv_sem=b_recv.at[z],
            device_id={"seq": k * PLANE + p},
            device_id_type=MESH,
        )

    def send_later(k, _):
        to_later(k).start()
        return 0

    lax.fori_loop(z + 1, depth, send_later, 0)

    held[...] = jnp.zeros_like(held)

    def from_earlier(k, _):
        pltpu.make_async_remote_copy(
            src_ref=total,
            dst_ref=zall.at[k],
            send_sem=b_send.at[k],
            recv_sem=b_recv.at[k],
            device_id={"seq": s},
            device_id_type=MESH,
        ).wait_recv()
        held[...] = (mm(held[...], zall[k, 0:128]) + zall[k, 128:192].astype(F32)).astype(BF16)
        return 0

    lax.fori_loop(0, z, from_earlier, 0)
    carry = held[...]

    mine = pl.ds(pl.multiple_of(64 * core, 64), 64)

    def to_block(d):
        q = lax.rem(p + d, PLANE)
        return pltpu.make_async_remote_copy(
            src_ref=lead.at[d],
            dst_ref=state.at[y, mine],
            send_sem=c_send.at[d],
            recv_sem=c_recv.at[p],
            device_id={"seq": base + q},
            device_id_type=MESH,
        )

    for d in range(1, PLANE):
        q = lax.rem(p + d, PLANE)
        lead[d] = (mm(carry, pre[q, 0:128]) + pre[q, 128:192].astype(F32)).astype(BF16)
        to_block(d).start()
    state[y, mine, :] = (mm(carry, pre[p, 0:128]) + pre[p, 128:192].astype(F32)).astype(BF16)
    for k in range(PLANE):

        @pl.when(p != k)
        def _():
            pltpu.make_async_remote_copy(
                src_ref=lead.at[0],
                dst_ref=state.at[k // 2, pl.ds(64 * (k % 2), 64)],
                send_sem=c_send.at[0],
                recv_sem=c_recv.at[k],
                device_id={"seq": s},
                device_id_type=MESH,
            ).wait_recv()

    heads = z_ref.shape[0]
    for i in range(heads):
        lanes = slice(i * 128, (i + 1) * 128)
        attended = o_ref[:, lanes] + mm(r_ref[:, lanes], state[i], ((1,), (1,)))
        scale = lax.rsqrt(jnp.mean(attended * attended, axis=1, keepdims=True) + 1e-05)
        normed[:, lanes] = (attended * scale * gain_ref[...] * gate_ref[:, lanes]).astype(BF16)

    rows = out_ref.shape[0]
    half = rows // 2
    far = lax.rem(h + 2, 4)

    def partial(owner):
        at = pl.ds(pl.multiple_of(owner * rows, 16), rows)
        return jnp.dot(normed[at, :], w_ref[...], preferred_element_type=F32)

    def piece(k, src, dst, target):
        return pltpu.make_async_remote_copy(
            src_ref=src,
            dst_ref=dst,
            send_sem=d_send.at[k],
            recv_sem=d_recv.at[k],
            device_id={"head": target},
            device_id_type=MESH,
        )

    top, low = pl.ds(0, half), pl.ds(half, half)
    part[0] = partial(far).astype(BF16)
    far_right = piece(0, part.at[0, top], inbox.at[0, top], right)
    far_left = piece(1, part.at[0, low], inbox.at[0, low], left)
    far_right.start()
    far_left.start()
    sums[0] = partial(right)
    part[1, low] = sums[0, low].astype(BF16)
    right_low = piece(2, part.at[1, low], inbox.at[1, low], right)
    right_low.start()
    sums[1] = partial(left)
    part[2, top] = sums[1, top].astype(BF16)
    left_top = piece(3, part.at[2, top], inbox.at[2, top], left)
    left_top.start()
    far_right.wait_recv()
    part[1, top] = (sums[0, top] + inbox[0, top].astype(F32)).astype(BF16)
    right_top = piece(4, part.at[1, top], inbox.at[1, top], right)
    right_top.start()
    far_left.wait_recv()
    part[2, low] = (sums[1, low] + inbox[0, low].astype(F32)).astype(BF16)
    left_low = piece(5, part.at[2, low], inbox.at[2, low], left)
    left_low.start()
    own = partial(h)
    right_low.wait_recv()
    left_top.wait_recv()
    right_top.wait_recv()
    left_low.wait_recv()
    out_ref[...] = (own + inbox[1].astype(F32) + inbox[2].astype(F32)).astype(BF16)

    for copy in (far_right, far_left, right_low, left_top, right_top, left_low):
        copy.wait_send()
    for d in range(1, PLANE):
        to_owner(d).wait_send()
        to_block(d).wait_send()

    def sent(k, _):
        to_later(k).wait_send()
        return 0

    lax.fori_loop(z + 1, depth, sent, 0)


def finish(depth, z, o, r, gate, gain, w):
    vmem = pl.BlockSpec(memory_space=pltpu.VMEM)
    rows, width = o.shape[0] // 4, w.shape[1]
    dma = pltpu.SemaphoreType.DMA
    return pl.pallas_call(
        functools.partial(finish_kernel, depth),
        name="finish",
        out_shape=jax.ShapeDtypeStruct((rows, width), BF16),
        in_specs=[vmem] * 6,
        out_specs=vmem,
        scratch_shapes=[
            pltpu.VMEM((PLANE, 192, 128), BF16),
            pltpu.VMEM((PLANE, 192, 128), BF16),
            pltpu.VMEM((192, 128), BF16),
            pltpu.VMEM((depth, 192, 128), BF16),
            pltpu.VMEM((64, 128), BF16),
            pltpu.VMEM((PLANE, 64, 128), BF16),
            pltpu.VMEM((4, 128, 128), BF16),
            pltpu.VMEM(o.shape, BF16),
            pltpu.VMEM((3, rows, width), BF16),
            pltpu.VMEM((2, rows, width), F32),
            pltpu.VMEM((3, rows, width), BF16),
            dma((PLANE,)), dma((PLANE,)), dma((depth,)), dma((depth,)),
            dma((PLANE,)), dma((PLANE,)), dma((6,)), dma((6,)),
        ],
        compiler_params=pltpu.CompilerParams(
            collective_id=1, has_side_effects=True, vmem_limit_bytes=56 << 20
        ),
    )(z, o, r, gate, gain, w)


def solution(mesh):
    seq_size = mesh.shape["seq"]
    span = span_matrix()

    def shards(
        hidden_in, qkv_weight, conv_weight, decay_log, dt_bias, decay_down, decay_up,
        beta_weight, gate_down, gate_up, norm_gain, out_weight,
    ):
        xg = gather(seq_size, hidden_in)
        o, r, gate, z = block(
            xg,
            jnp.transpose(qkv_weight, (1, 0, 2)),
            decay_down,
            gate_down,
            beta_weight.T,
            decay_up,
            gate_up,
            conv_weight,
            decay_log,
            dt_bias.reshape(1, -1),
            jnp.asarray(span, BF16),
        )
        return finish(
            seq_size // PLANE, z, o, r, gate, norm_gain.reshape(1, -1), out_weight
        )

    rows = P(("seq", "head"), None)
    return jax.shard_map(
        shards,
        mesh=mesh,
        in_specs=(
            rows, P(None, None, "head"), P(None, None, "head"), P("head"), P("head"), P(),
            P(None, "head"), P(None, "head"), P(), P(None, "head"), P(), P("head", None),
        ),
        out_specs=rows,
        check_vma=False,
    )
```

time: 469 us -> 81 us (0.17)
  blocking collectives: 321 us -> 0 us
  Pallas kernels: 0 us -> 79.2 us
  matrix products: 73 us -> 0 us
  waiting for transfers between devices: 24.7 us -> 0 us
  local copies, waits for them, and re-layouts: 21.3 us -> 1.69 us
  between operations: 13.8 us -> 0.02 us
  other arithmetic: 7.51 us -> 0 us
    all_gather x24 -> x0, blocking collectives: 311 us -> none  [carried_in(): lax.all_gather(part.astype(kind), axis)]
    pallas_call x0 -> x3, Pallas kernels: none -> 79.2 us  [the longest x1 44.6 us: finish(): pl.pallas_call(functools.partial(finish_kernel, depth), name='finish', ou...]
    dot_general x194 -> x0, matrix products: 73 us -> none  [the longest x72 25.7 us: product(): return jnp.einsum('hij,hjk->hik', left, right, precision=exact_precision)]
    all_gather x2 -> x0, waiting for transfers between devices: 18.4 us -> none  [the longest x1 18.3 us: shards(): gathered = lax.all_gather(hidden_in, 'head', axis=0, tiled=True)]
    all_to_all x1 -> x0, blocking collectives: 10.2 us -> none  [shards(): lax.all_to_all(normed, 'head', split_axis=0, concat_axis=1, tiled=True)]
    unnamed x29 -> x1, local copies, waits for them, and re-layouts: 10.7 us -> 1.69 us
    ppermute x1 -> x0, waiting for transfers between devices: 4.94 us -> none  [passed_along(): return lax.ppermute(block, axis, route)]
    convert_element_type x12 -> x0, other arithmetic: 4.94 us -> none  [the longest x1 2.39 us: shards(): convolved = jax.nn.silu(convolved).astype(jnp.bfloat16)]
  transfers between devices with their start and end apart: 3 -> 0, of which waited for: 2 -> 0; matrix products, arithmetic and copies ran while one was open for 20% -> 0% of each run, Pallas kernels for 0% -> 0%
where the time goes in v1:
time: 81 us; the launch traced here: 80.9 us
  Pallas kernels  79.2 us (98%)
  local copies, waits for them, and re-layouts  1.69 us (2%)
    pallas_call x1, Pallas kernels, finish(): pl.pallas_call(functools.partial(finish_kernel, depth), name='finish', ou...  44.6 us
    pallas_call x1, Pallas kernels, block(): pl.pallas_call(block_kernel, name='block', out_shape=(jax.ShapeDtypeStruc...  19.6 us
    pallas_call x1, Pallas kernels, gather(): pl.pallas_call(functools.partial(gather_kernel, seq_size), name='gather',...  15 us
    unnamed x1, local copies, waits for them, and re-layouts  1.69 us

profile of v1, /device:TPU:192, one launch (start us, length us, event | category | flops | bytes accessed | tf_op | source)
XLA Modules:
  0.0 80.9 jit_solution(2852924038174354750)
XLA Ops:
  0.0 15.0 %gather.1.xg_ref = bf16[272,2304]{1,0:T(8,128)(2,1)} custom-call(bf16[64,2304]{1,0:T(8,128)(2,1)} %x_ref.1), custom_call_target="tpu_custom_call" | custom-call | tf_op jit(solution)/shard_map/gather/pallas_call | solution.py:157
  15.0 19.6 %block.1 = (f32[256,512]{1,0:T(8,128)}, bf16[256,512]{1,0:T(8,128)(2,1)}, f32[256,512]{1,0:T(8,128)}, bf16[4,256,128]{2,1,0:T(8,128)(2,1)}) custom-call(bf16[272,2304]{1,0:T(8,128)(2,1)} %gather.1.xg_ref, bf16[3,2304,512]{2,1,0:T(8,128)(2,1)} %bitcast.4, bf16[2304,128]{1,0:T(8,128)(2,1)} %down_ref.1, bf16[2304,128]{1,0:T(8,128)(2,1)} %gdown_ref.1, ...), custom_call_target="tpu_custom_call" | custom-call | tf_op jit(solution)/shard_map/block/pallas_call | solution.py:299
  34.6 44.6 %finish.1 = bf16[64,2304]{1,0:T(8,128)(2,1)} custom-call(bf16[4,256,128]{2,1,0:T(8,128)(2,1)} %get-tuple-element.9.z_ref, f32[256,512]{1,0:T(8,128)} %get-tuple-element.10.o_ref, bf16[256,512]{1,0:T(8,128)(2,1)} %get-tuple-element.11.r_ref, f32[256,512]{1,0:T(8,128)} %get-tuple-element.12.gate_ref, f32[1,128]{1,0:T(1,128)} %bitcast.7, bf16[512,2304]{1,0:T(8,128)(2,1)} %w_ref.1), custom_call_target="tpu_custom_call" | custom-call | tf_op jit(solution)/shard_map/finish/pallas_call | solution.py:537
  79.2 1.7 %copy.15 = bf16[64,2304]{1,0:T(8,128)(2,1)} copy(bf16[64,2304]{1,0:T(8,128)(2,1)} %finish.1) | data formatting | bytes 589824

commit v2 on v1

v2 whole, which is shorter than its diff:
```python
import functools

import jax
import jax.numpy as jnp
import numpy as np
from jax import lax
from jax.experimental import pallas as pl
from jax.experimental.pallas import tpu as pltpu
from jax.sharding import PartitionSpec as P

F32 = jnp.float32
BF16 = jnp.bfloat16
MESH = pl.DeviceIdType.MESH

HALO = 16
EDGE = 8
HALF = 128
LEVELS = (1, 2, 4, 8, 16, 32, 64)
PLANE = 8


def span_matrix():
    r, i = np.arange(HALF)[:, None], np.arange(HALF)[None, :]
    rows = []
    for size in LEVELS:
        middle = (r // (2 * size)) * 2 * size + size - 1
        late = (r % (2 * size)) >= size
        rows.append(np.where(late, (i > middle) & (i <= r), (i > r) & (i <= middle)))
    rows.append(i <= r)
    rows.append(i > r)
    spans = np.concatenate(rows, axis=0)
    return np.concatenate([spans, spans], axis=1).astype(np.float32)


def mm(a, b, dims=((1,), (0,))):
    return lax.dot_general(
        a.astype(BF16), b.astype(BF16), (dims, ((), ())), preferred_element_type=F32
    )


def sigmoid(v):
    return 1.0 / (1.0 + jnp.exp(-v))


def kernel(
    depth, x_hbm, w_hbm, down_hbm, gdown_hbm, beta_hbm, up_ref, gup_ref, conv_ref, dlog_ref,
    bias_ref, span_hbm, gain_ref, ow_hbm, out_ref,
    x_ref, w_ref, dg_ref, beta_ref, span_ref, ow_ref,
    proj_ref, low_ref, strength_ref, q_ref, k_ref, v_ref, e_ref, o_ref, r_ref, gate_ref, z_ref,
    zin, pre, total, zall, held, lead, state, normed, part, sums, inbox,
    l_sem, x_send, x_recv, e_sem,
    a_send, a_recv, b_send, b_recv, c_send, c_recv, d_send, d_recv,
):
    s = lax.axis_index("seq")
    h = lax.axis_index("head")
    z = lax.div(s, PLANE)
    p = lax.rem(s, PLANE)
    y, core = lax.div(p, 2), lax.rem(p, 2)
    base = z * PLANE
    right, left, far = lax.rem(h + 1, 4), lax.rem(h + 3, 4), lax.rem(h + 2, 4)
    owner = core == 0
    sends_edge = jnp.logical_and(h == 3, s < depth * PLANE - 1)
    rows = x_hbm.shape[0]
    half = rows // 2
    count = 4 * rows
    width = w_ref.shape[2]
    heads = width // 128

    barrier = pltpu.get_barrier_semaphore()
    pl.semaphore_signal(barrier, 1, device_id={"head": right}, device_id_type=MESH)
    pl.semaphore_signal(barrier, 1, device_id={"head": left}, device_id_type=MESH)

    @pl.when(s > 0)
    def _():
        pl.semaphore_signal(
            barrier, 1, device_id={"seq": s - 1, "head": 3}, device_id_type=MESH
        )

    for d in range(1, PLANE):
        pl.semaphore_signal(
            barrier, 1, device_id={"seq": base + lax.rem(p + d, PLANE)}, device_id_type=MESH
        )

    def greet(k, _):
        pl.semaphore_signal(barrier, 1, device_id={"seq": k * PLANE + p}, device_id_type=MESH)
        return 0

    lax.fori_loop(0, z, greet, 0)

    loads = [
        pltpu.make_async_copy(src, dst, l_sem.at[k])
        for k, (src, dst) in enumerate(
            [
                (x_hbm, x_ref.at[pl.ds(0, rows)]),
                (w_hbm.at[0], w_ref.at[0]),
                (w_hbm.at[1], w_ref.at[1]),
                (w_hbm.at[2], w_ref.at[2]),
                (down_hbm, dg_ref.at[:, pl.ds(0, 128)]),
                (gdown_hbm, dg_ref.at[:, pl.ds(128, 128)]),
                (beta_hbm, beta_ref),
                (span_hbm, span_ref),
                (ow_hbm, ow_ref),
            ]
        )
    ]
    for load in loads:
        load.start()
    x_ref[count + EDGE :, :] = jnp.zeros((HALO - EDGE, x_ref.shape[1]), BF16)

    @pl.when(s == 0)
    def _():
        x_ref[count : count + EDGE, :] = jnp.zeros((EDGE, x_ref.shape[1]), BF16)

    pl.semaphore_wait(
        barrier, 2 + PLANE - 1 + (depth - 1 - z) + jnp.where(sends_edge, 4, 0)
    )

    def piece(src, slot, half_at, target, k):
        return pltpu.make_async_remote_copy(
            src_ref=src,
            dst_ref=x_ref.at[pl.ds(slot * rows + half_at * half, half)],
            send_sem=x_send.at[k],
            recv_sem=x_recv.at[k],
            device_id={"head": target},
            device_id_type=MESH,
        )

    def rows_at(slot, half_at):
        return x_ref.at[pl.ds(slot * rows + half_at * half, half)]

    mine = [x_hbm.at[pl.ds(0, half)], x_hbm.at[pl.ds(half, half)]]
    moves = [
        piece(mine[0], 1, 0, right, 0),
        piece(mine[1], 2, 1, left, 1),
        piece(mine[1], 1, 1, right, 2),
        piece(mine[0], 2, 0, left, 3),
        piece(rows_at(1, 0), 3, 0, right, 4),
        piece(rows_at(2, 1), 3, 1, left, 5),
    ]
    for move in moves[:4]:
        move.start()

    def edge(target):
        return pltpu.make_async_remote_copy(
            src_ref=x_hbm.at[pl.ds(rows - EDGE, EDGE)],
            dst_ref=x_ref.at[pl.ds(count, EDGE)],
            send_sem=e_sem.at[target],
            recv_sem=e_sem.at[4],
            device_id={"seq": s + 1, "head": target},
            device_id_type=MESH,
        )

    @pl.when(sends_edge)
    def _():
        for target in range(4):
            edge(target).start()

    moves[0].wait_recv()
    moves[4].start()
    moves[1].wait_recv()
    moves[5].start()
    for load in loads[:7]:
        load.wait()
    moves[2].wait_recv()
    moves[3].wait_recv()

    def project(first, slots):
        size = len(slots) * rows
        at = [pl.ds(pl.multiple_of(slot * rows, 16), rows) for slot in slots]
        some = x_ref[first : first + size, :]
        both = jnp.dot(some, dg_ref[...], preferred_element_type=F32).astype(BF16)
        force = sigmoid(
            lax.dot_general(
                some, beta_ref[...], (((1,), (1,)), ((), ())), preferred_element_type=F32
            )
        )
        for n, where in enumerate(at):
            low_ref[where, :] = both[n * rows : (n + 1) * rows]
            strength_ref[where, :] = force[n * rows : (n + 1) * rows]

    def project_qkv(c, first, slots, tail):
        size = len(slots) * rows
        some = x_ref[first : first + size + tail, :]
        got = jnp.dot(some, w_ref[c], preferred_element_type=F32).astype(BF16).astype(F32)
        for n, slot in enumerate(slots):
            at = pl.ds(pl.multiple_of(HALO + slot * rows, 16), rows)
            proj_ref[c, at, :] = got[n * rows : (n + 1) * rows]
        if tail:
            proj_ref[c, HALO - EDGE : HALO, :] = got[size : size + EDGE]

    near = (h, left, right)
    project(0, near)
    for c in range(3):
        project_qkv(c, 0, near, 0)
    moves[4].wait_recv()
    moves[5].wait_recv()

    @pl.when(s > 0)
    def _():
        edge(0).wait_recv()

    project(3 * rows, (far,))
    for c in range(3):
        project_qkv(c, 3 * rows, (far,), HALO)

    raw = jnp.dot(low_ref[:, 0:128], up_ref[...], preferred_element_type=F32) + bias_ref[...]
    soft = jnp.maximum(raw, 0.0) + jnp.log1p(jnp.exp(-jnp.abs(raw)))
    rate = jnp.concatenate(
        [jnp.exp(jnp.full((1, 128), dlog_ref[i], F32)) for i in range(heads)], axis=1
    )
    log_decay = -rate * soft
    loads[7].wait()
    for c in range(2):
        piece_of = log_decay[c * HALF : (c + 1) * HALF]
        top = piece_of.astype(BF16)
        rest = (piece_of - top.astype(F32)).astype(BF16)
        e_ref[c] = jnp.exp(
            jnp.dot(
                span_ref[...], jnp.concatenate([top, rest], axis=0), preferred_element_type=F32
            )
        )
    gate_ref[...] = sigmoid(
        jnp.dot(low_ref[:, 128:256], gup_ref[...], preferred_element_type=F32)
    )
    beta = strength_ref[...]

    for c, target in enumerate((q_ref, k_ref, v_ref)):
        taps = conv_ref[c].astype(F32)
        mixed = proj_ref[c, pl.ds(HALO - 3, count), :] * taps[0:1]
        for i in range(1, 4):
            mixed = mixed + proj_ref[c, pl.ds(HALO - 3 + i, count), :] * taps[i : i + 1]
        mixed = (mixed * sigmoid(mixed)).astype(BF16).astype(F32)
        if c == 2:
            target[...] = mixed
            continue
        for i in range(heads):
            lanes = slice(i * 128, (i + 1) * 128)
            u = mixed[:, lanes]
            scale = lax.rsqrt(jnp.sum(u * u, axis=1, keepdims=True) + 1e-06)
            if c == 0:
                scale = scale * (128**-0.5)
            target[:, lanes] = u * scale

    t = lax.broadcasted_iota(jnp.int32, (HALF, HALF), 0)
    j = lax.broadcasted_iota(jnp.int32, (HALF, HALF), 1)
    row = lax.broadcasted_iota(jnp.int32, (HALF, 128), 0)
    masks = [
        ((t ^ j) >= size) & ((t ^ j) < 2 * size) & (t > j) for size in LEVELS
    ]
    diagonal = t == j

    pairs = [(i, c) for i in range(heads) for c in range(2)]
    lanes_of = [slice(i * 128, (i + 1) * 128) for i in range(heads)]
    rows_of = [slice(c * HALF, (c + 1) * HALF) for c in range(2)]
    strength = {
        (i, c): jnp.broadcast_to(beta[rows_of[c], i : i + 1], (HALF, 128)) for i, c in pairs
    }
    attend, inverse = {}, {}
    for i, c in pairs:
        kc, qc = k_ref[rows_of[c], lanes_of[i]], q_ref[rows_of[c], lanes_of[i]]
        own = jnp.sum(qc * kc, axis=1, keepdims=True) * strength[i, c]
        attend[i, c] = jnp.where(diagonal, own, 0.0)
        inverse[i, c] = jnp.where(diagonal, 1.0, 0.0)
    for n, size in enumerate(LEVELS):
        for i, c in pairs:
            kc, qc = k_ref[rows_of[c], lanes_of[i]], q_ref[rows_of[c], lanes_of[i]]
            fade = e_ref[c, n * HALF : (n + 1) * HALF, lanes_of[i]]
            late = (row & size) != 0
            kx = (kc * fade * jnp.where(late, 1.0, strength[i, c])).astype(BF16)
            qx = (qc * fade).astype(BF16)
            both = mm(jnp.concatenate([kx, qx], axis=0), kx, ((1,), (1,)))
            mixing = jnp.where(masks[n], both[:HALF], 0.0)
            attend[i, c] = jnp.where(masks[n], both[HALF:], attend[i, c])
            if size == 1:
                inverse[i, c] = inverse[i, c] - mixing
            else:
                own = inverse[i, c].astype(BF16)
                inverse[i, c] = inverse[i, c] - mm(mm(own, mixing), own)

    def to_owner(i):
        return pltpu.make_async_remote_copy(
            src_ref=z_ref.at[i],
            dst_ref=zin.at[p],
            send_sem=a_send.at[i],
            recv_sem=a_recv.at[p],
            device_id={"seq": base + 2 * i},
            device_id_type=MESH,
        )

    n = len(LEVELS)
    for i in range(heads):
        lanes = lanes_of[i]
        rise = [e_ref[c, n * HALF : (n + 1) * HALF, lanes] for c in range(2)]
        fall = [e_ref[c, (n + 1) * HALF : (n + 2) * HALF, lanes] for c in range(2)]
        whole = [part[HALF - 1 : HALF] for part in rise]
        k = [k_ref[rows_of[c], lanes] for c in range(2)]
        q = [q_ref[rows_of[c], lanes] for c in range(2)]
        k_rise = [k[c] * rise[c] for c in range(2)]
        q_rise = [q[c] * rise[c] for c in range(2)]
        k_fall = [k[c] * fall[c] * strength[i, c] for c in range(2)]
        cross = mm(jnp.concatenate([k_rise[1], q_rise[1]], axis=0), k_fall[0], ((1,), (1,)))
        first = mm(
            inverse[i, 0], jnp.concatenate([v_ref[rows_of[0], lanes], k_rise[0]], axis=1)
        ).astype(BF16)
        second = jnp.concatenate([v_ref[rows_of[1], lanes], k_rise[1] * whole[0]], axis=1)
        second = mm(inverse[i, 1], second - mm(cross[:HALF], first)).astype(BF16)
        out = [mm(attend[i, 0], first), mm(cross[HALF:], first) + mm(attend[i, 1], second)]
        for c in range(2):
            o_ref[rows_of[c], lanes] = out[c][:, :128]
        r_ref[rows_of[0], lanes] = (q_rise[0] - out[0][:, 128:]).astype(BF16)
        r_ref[rows_of[1], lanes] = (q_rise[1] * whole[0] - out[1][:, 128:]).astype(BF16)
        stop = jnp.concatenate([k_fall[0] * whole[1], k_fall[1]], axis=0).astype(BF16)
        maps = mm(jnp.concatenate([first, second], axis=0), stop, ((0,), (0,)))
        move = jnp.where(diagonal, whole[0] * whole[1], 0.0) - maps[128:]
        z_ref[i, 0:128] = move.astype(BF16)
        z_ref[i, 128:256] = maps[:128].astype(BF16)

        @pl.when(p != 2 * i)
        def _():
            to_owner(i).start()

    def to_later(k):
        return pltpu.make_async_remote_copy(
            src_ref=total,
            dst_ref=zall.at[z],
            send_sem=b_send.at[k],
            recv_sem=b_recv.at[z],
            device_id={"seq": k * PLANE + p},
            device_id_type=MESH,
        )

    def to_block(q):
        return pltpu.make_async_remote_copy(
            src_ref=lead.at[q],
            dst_ref=state.at[y],
            send_sem=c_send.at[q],
            recv_sem=c_recv.at[y],
            device_id={"seq": base + q},
            device_id_type=MESH,
        )

    def send_later(k, _):
        to_later(k).start()
        return 0

    def from_earlier(k, _):
        pltpu.make_async_remote_copy(
            src_ref=total,
            dst_ref=zall.at[k],
            send_sem=b_send.at[k],
            recv_sem=b_recv.at[k],
            device_id={"seq": s},
            device_id_type=MESH,
        ).wait_recv()
        held[...] = (mm(held[...], zall[k, 0:128]) + zall[k, 128:256].astype(F32)).astype(BF16)
        return 0

    @pl.when(owner)
    def _():
        zin[p] = z_ref[y]
        for k in range(PLANE):

            @pl.when(p != k)
            def _():
                pltpu.make_async_remote_copy(
                    src_ref=z_ref.at[0],
                    dst_ref=zin.at[k],
                    send_sem=a_send.at[0],
                    recv_sem=a_recv.at[k],
                    device_id={"seq": s},
                    device_id_type=MESH,
                ).wait_recv()

            if k == 0:
                so_far = zin[0]
            else:
                step = mm(so_far, zin[k, 0:128])
                so_far = jnp.concatenate(
                    [
                        step[:128].astype(BF16),
                        (step[128:] + zin[k, 128:256].astype(F32)).astype(BF16),
                    ],
                    axis=0,
                )
            if k < PLANE - 1:
                pre[k + 1] = so_far
            else:
                total[...] = so_far
        lax.fori_loop(z + 1, depth, send_later, 0)
        held[...] = jnp.zeros_like(held)
        lax.fori_loop(0, z, from_earlier, 0)
        carry = held[...]
        for q in range(PLANE):
            if q == 0:
                lead[0] = carry
            else:
                lead[q] = (mm(carry, pre[q, 0:128]) + pre[q, 128:256].astype(F32)).astype(BF16)

            @pl.when(p != q)
            def _():
                to_block(q).start()

        state[y] = lead[p]

    def states_in(i):
        @pl.when(p != 2 * i)
        def _():
            pltpu.make_async_remote_copy(
                src_ref=lead.at[0],
                dst_ref=state.at[i],
                send_sem=c_send.at[0],
                recv_sem=c_recv.at[i],
                device_id={"seq": s},
                device_id_type=MESH,
            ).wait_recv()

    for i in range(heads):
        states_in(i)
        lanes = lanes_of[i]
        attended = o_ref[:, lanes] + mm(r_ref[:, lanes], state[i], ((1,), (1,)))
        scale = lax.rsqrt(jnp.mean(attended * attended, axis=1, keepdims=True) + 1e-05)
        normed[:, lanes] = (attended * scale * gain_ref[...] * gate_ref[:, lanes]).astype(BF16)
    loads[8].wait()


    def partial(to):
        at = pl.ds(pl.multiple_of(to * rows, 16), rows)
        return jnp.dot(normed[at, :], ow_ref[...], preferred_element_type=F32)

    def pass_on(k, src, dst, target):
        return pltpu.make_async_remote_copy(
            src_ref=src,
            dst_ref=dst,
            send_sem=d_send.at[k],
            recv_sem=d_recv.at[k],
            device_id={"head": target},
            device_id_type=MESH,
        )

    top, low = pl.ds(0, half), pl.ds(half, half)
    part[0] = partial(far).astype(BF16)
    far_right = pass_on(0, part.at[0, top], inbox.at[0, top], right)
    far_left = pass_on(1, part.at[0, low], inbox.at[0, low], left)
    far_right.start()
    far_left.start()
    sums[0] = partial(right)
    part[1, low] = sums[0, low].astype(BF16)
    right_low = pass_on(2, part.at[1, low], inbox.at[1, low], right)
    right_low.start()
    sums[1] = partial(left)
    part[2, top] = sums[1, top].astype(BF16)
    left_top = pass_on(3, part.at[2, top], inbox.at[2, top], left)
    left_top.start()
    far_right.wait_recv()
    part[1, top] = (sums[0, top] + inbox[0, top].astype(F32)).astype(BF16)
    right_top = pass_on(4, part.at[1, top], inbox.at[1, top], right)
    right_top.start()
    far_left.wait_recv()
    part[2, low] = (sums[1, low] + inbox[0, low].astype(F32)).astype(BF16)
    left_low = pass_on(5, part.at[2, low], inbox.at[2, low], left)
    left_low.start()
    own = partial(h)
    right_low.wait_recv()
    left_top.wait_recv()
    right_top.wait_recv()
    left_low.wait_recv()
    out_ref[...] = (own + inbox[1].astype(F32) + inbox[2].astype(F32)).astype(BF16)

    for copy in (far_right, far_left, right_low, left_top, right_top, left_low):
        copy.wait_send()
    for move in moves:
        move.wait_send()

    @pl.when(sends_edge)
    def _():
        for target in range(4):
            edge(target).wait_send()

    for i in range(heads):

        @pl.when(p != 2 * i)
        def _():
            to_owner(i).wait_send()

    def sent(k, _):
        to_later(k).wait_send()
        return 0

    @pl.when(owner)
    def _():
        lax.fori_loop(z + 1, depth, sent, 0)
        for q in range(PLANE):

            @pl.when(p != q)
            def _():
                to_block(q).wait_send()


def layer(depth, x, w, down, gdown, beta, up, gup, conv, dlog, bias, span, gain, ow):
    vmem = pl.BlockSpec(memory_space=pltpu.VMEM)
    smem = pl.BlockSpec(memory_space=pltpu.SMEM)
    hbm = pl.BlockSpec(memory_space=pl.ANY)
    rows, model = x.shape
    count, width = 4 * rows, w.shape[2]
    heads = width // 128
    dma = pltpu.SemaphoreType.DMA
    return pl.pallas_call(
        functools.partial(kernel, depth),
        name="layer",
        out_shape=jax.ShapeDtypeStruct((rows, model), BF16),
        in_specs=[hbm] * 5 + [vmem] * 3 + [smem, vmem, hbm, vmem, hbm],
        out_specs=vmem,
        scratch_shapes=[
            pltpu.VMEM((count + HALO, model), BF16),
            pltpu.VMEM(w.shape, BF16),
            pltpu.VMEM((model, 256), BF16),
            pltpu.VMEM(beta.shape, BF16),
            pltpu.VMEM(span.shape, BF16),
            pltpu.VMEM(ow.shape, BF16),
            pltpu.VMEM((3, HALO + count, width), F32),
            pltpu.VMEM((count, 256), BF16),
            pltpu.VMEM((count, heads), F32),
            pltpu.VMEM((count, width), F32),
            pltpu.VMEM((count, width), F32),
            pltpu.VMEM((count, width), F32),
            pltpu.VMEM((2, (len(LEVELS) + 2) * HALF, width), F32),
            pltpu.VMEM((count, width), F32),
            pltpu.VMEM((count, width), BF16),
            pltpu.VMEM((count, width), F32),
            pltpu.VMEM((heads, 256, 128), BF16),
            pltpu.VMEM((PLANE, 256, 128), BF16),
            pltpu.VMEM((PLANE, 256, 128), BF16),
            pltpu.VMEM((256, 128), BF16),
            pltpu.VMEM((depth, 256, 128), BF16),
            pltpu.VMEM((128, 128), BF16),
            pltpu.VMEM((PLANE, 128, 128), BF16),
            pltpu.VMEM((heads, 128, 128), BF16),
            pltpu.VMEM((count, width), BF16),
            pltpu.VMEM((3, rows, model), BF16),
            pltpu.VMEM((2, rows, model), F32),
            pltpu.VMEM((3, rows, model), BF16),
            dma((9,)), dma((6,)), dma((6,)), dma((5,)),
            dma((heads,)), dma((PLANE,)), dma((depth,)), dma((depth,)),
            dma((PLANE,)), dma((heads,)), dma((6,)), dma((6,)),
        ],
        compiler_params=pltpu.CompilerParams(
            collective_id=0, has_side_effects=True, vmem_limit_bytes=56 << 20
        ),
    )(x, w, down, gdown, beta, up, gup, conv, dlog, bias, span, gain, ow)


def solution(mesh):
    seq_size = mesh.shape["seq"]
    span = span_matrix()

    def shards(
        hidden_in, qkv_weight, conv_weight, decay_log, dt_bias, decay_down, decay_up,
        beta_weight, gate_down, gate_up, norm_gain, out_weight,
    ):
        return layer(
            seq_size // PLANE,
            hidden_in,
            jnp.transpose(qkv_weight, (1, 0, 2)),
            decay_down,
            gate_down,
            beta_weight.T,
            decay_up,
            gate_up,
            conv_weight,
            decay_log,
            dt_bias.reshape(1, -1),
            jnp.asarray(span, BF16),
            norm_gain.reshape(1, -1),
            out_weight,
        )

    rows = P(("seq", "head"), None)
    return jax.shard_map(
        shards,
        mesh=mesh,
        in_specs=(
            rows, P(None, None, "head"), P(None, None, "head"), P("head"), P("head"), P(),
            P(None, "head"), P(None, "head"), P(), P(None, "head"), P(), P("head", None),
        ),
        out_specs=rows,
        check_vma=False,
    )
```

time: 81 us -> 67.6 us (0.83)
  Pallas kernels: 79.2 us -> 65.4 us
    pallas_call x3 -> x1, Pallas kernels: 79.2 us -> 65.4 us  [layer(): pl.pallas_call(functools.partial(kernel, depth), name='layer', out_shape=...]
where the time goes in v2:
time: 67.6 us; the launch traced here: 67.1 us
  Pallas kernels  65.4 us (97%)
  local copies, waits for them, and re-layouts  1.69 us (2%)
    pallas_call x1, Pallas kernels, layer(): pl.pallas_call(functools.partial(kernel, depth), name='layer', out_shape=...  65.4 us
    unnamed x1, local copies, waits for them, and re-layouts  1.69 us

profile of v2, /device:TPU:192, one launch (start us, length us, event | category | flops | bytes accessed | tf_op | source)
XLA Modules:
  0.0 67.1 jit_solution(1636384787797460498)
XLA Ops:
  0.0 65.4 %layer.1 = bf16[64,2304]{1,0:T(8,128)(2,1)} custom-call(bf16[64,2304]{1,0:T(8,128)(2,1)} %x_hbm.1, bf16[3,2304,512]{2,1,0:T(8,128)(2,1)} %bitcast.4, bf16[2304,128]{1,0:T(8,128)(2,1)} %down_hbm.1, bf16[2304,128]{1,0:T(8,128)(2,1)} %gdown_hbm.1, bf16[4,2304]{1,0:T(4,128)(2,1)} %bitcast.5, bf16[128,512]{1,0:T(8,128)(2,1)} %up_ref.1, bf16[128,512]{1,0:T(8,128)(2,1)} %gup_ref.1, ...), custom_call_target="tpu_custom_call" | custom-call | tf_op jit(solution)/shard_map/layer/pallas_call | solution.py:507
  65.4 1.7 %copy.15 = bf16[64,2304]{1,0:T(8,128)(2,1)} copy(bf16[64,2304]{1,0:T(8,128)(2,1)} %layer.1) | data formatting | bytes 589824

commit v3 on v2

--- a/solution.py
+++ b/solution.py
@@ -17,6 +17,7 @@
 HALF = 128
 LEVELS = (1, 2, 4, 8, 16, 32, 64)
 PLANE = 8
+GROUP = 4
 
 
 def span_matrix():
@@ -47,8 +48,8 @@
     bias_ref, span_hbm, gain_ref, ow_hbm, out_ref,
     x_ref, w_ref, dg_ref, beta_ref, span_ref, ow_ref,
     proj_ref, low_ref, strength_ref, q_ref, k_ref, v_ref, e_ref, o_ref, r_ref, gate_ref, z_ref,
-    zin, pre, total, zall, held, lead, state, normed, part, sums, inbox,
-    l_sem, x_send, x_recv, e_sem,
+    mix_ref, attend_ref, zin, pre, total, zall, chain, link, held, lead, state, normed, part, sums, inbox,
+    l_sem, x_send, x_recv, e_sem, f_sem,
     a_send, a_recv, b_send, b_recv, c_send, c_recv, d_send, d_recv,
 ):
     s = lax.axis_index("seq")
@@ -59,7 +60,10 @@
     base = z * PLANE
     right, left, far = lax.rem(h + 1, 4), lax.rem(h + 3, 4), lax.rem(h + 2, 4)
     owner = core == 0
-    sends_edge = jnp.logical_and(h == 3, s < depth * PLANE - 1)
+    group, rank = lax.div(z, GROUP), lax.rem(z, GROUP)
+    feeds = jnp.logical_and(group == 0, jnp.logical_or(rank == 0, rank == GROUP - 1))
+    has_next = s < depth * PLANE - 1
+    edge_from = jnp.where(h == 1, 3, h)
     rows = x_hbm.shape[0]
     half = rows // 2
     count = 4 * rows
@@ -73,19 +77,37 @@
     @pl.when(s > 0)
     def _():
         pl.semaphore_signal(
-            barrier, 1, device_id={"seq": s - 1, "head": 3}, device_id_type=MESH
+            barrier, 1, device_id={"seq": s - 1, "head": edge_from}, device_id_type=MESH
         )
 
     for d in range(1, PLANE):
-        pl.semaphore_signal(
-            barrier, 1, device_id={"seq": base + lax.rem(p + d, PLANE)}, device_id_type=MESH
-        )
-
-    def greet(k, _):
-        pl.semaphore_signal(barrier, 1, device_id={"seq": k * PLANE + p}, device_id_type=MESH)
-        return 0
-
-    lax.fori_loop(0, z, greet, 0)
+        q = lax.rem(p + d, PLANE)
+
+        @pl.when(jnp.logical_or(owner, lax.rem(q, 2) == 0))
+        def _():
+            pl.semaphore_signal(barrier, 1, device_id={"seq": base + q}, device_id_type=MESH)
+
+    @pl.when(owner)
+    def _():
+        for d in range(1, GROUP):
+            other = group * GROUP + lax.rem(rank + d, GROUP)
+            pl.semaphore_signal(
+                barrier, 1, device_id={"seq": other * PLANE + p}, device_id_type=MESH
+            )
+
+        @pl.when(group == 1)
+        def _():
+            feeder = jnp.where(rank < 2, GROUP - 1, 0)
+            pl.semaphore_signal(
+                barrier, 1, device_id={"seq": feeder * PLANE + p}, device_id_type=MESH
+            )
+
+    greeted = (
+        2
+        + jnp.where(owner, PLANE - 1 + GROUP - 1, PLANE // 2)
+        + jnp.where(jnp.logical_and(owner, feeds), 2, 0)
+        + jnp.where(has_next, jnp.where(h == 3, 2, jnp.where(h == 1, 0, 1)), 0)
+    )
 
     loads = [
         pltpu.make_async_copy(src, dst, l_sem.at[k])
@@ -111,9 +133,7 @@
     def _():
         x_ref[count : count + EDGE, :] = jnp.zeros((EDGE, x_ref.shape[1]), BF16)
 
-    pl.semaphore_wait(
-        barrier, 2 + PLANE - 1 + (depth - 1 - z) + jnp.where(sends_edge, 4, 0)
-    )
+    pl.semaphore_wait(barrier, greeted)
 
     def piece(src, slot, half_at, target, k):
         return pltpu.make_async_remote_copy(
@@ -140,28 +160,39 @@
     for move in moves[:4]:
         move.start()
 
-    def edge(target):
+    def edge(k, src, target):
         return pltpu.make_async_remote_copy(
-            src_ref=x_hbm.at[pl.ds(rows - EDGE, EDGE)],
+            src_ref=src,
             dst_ref=x_ref.at[pl.ds(count, EDGE)],
-            send_sem=e_sem.at[target],
-            recv_sem=e_sem.at[4],
+            send_sem=e_sem.at[k],
+            recv_sem=e_sem.at[2],
             device_id={"seq": s + 1, "head": target},
             device_id_type=MESH,
         )
 
-    @pl.when(sends_edge)
-    def _():
-        for target in range(4):
-            edge(target).start()
-
+    last = pl.ds(rows - EDGE, EDGE)
+    edges = {
+        3: [edge(0, x_hbm.at[last], 3), edge(1, x_hbm.at[last], 1)],
+        0: [edge(0, x_ref.at[pl.ds(2 * rows - EDGE, EDGE)], 0)],
+        2: [edge(0, x_ref.at[pl.ds(3 * rows - EDGE, EDGE)], 2)],
+    }
+
+    def each_edge(head, act):
+        @pl.when(jnp.logical_and(h == head, has_next))
+        def _():
+            for copy in edges[head]:
+                act(copy)
+
+    each_edge(3, lambda copy: copy.start())
     moves[0].wait_recv()
     moves[4].start()
     moves[1].wait_recv()
     moves[5].start()
+    each_edge(2, lambda copy: copy.start())
     for load in loads[:7]:
         load.wait()
     moves[2].wait_recv()
+    each_edge(0, lambda copy: copy.start())
     moves[3].wait_recv()
 
     def project(first, slots):
@@ -197,7 +228,7 @@
 
     @pl.when(s > 0)
     def _():
-        edge(0).wait_recv()
+        edges[0][0].wait_recv()
 
     project(3 * rows, (far,))
     for c in range(3):
@@ -249,33 +280,8 @@
     ]
     diagonal = t == j
 
-    pairs = [(i, c) for i in range(heads) for c in range(2)]
     lanes_of = [slice(i * 128, (i + 1) * 128) for i in range(heads)]
     rows_of = [slice(c * HALF, (c + 1) * HALF) for c in range(2)]
-    strength = {
-        (i, c): jnp.broadcast_to(beta[rows_of[c], i : i + 1], (HALF, 128)) for i, c in pairs
-    }
-    attend, inverse = {}, {}
-    for i, c in pairs:
-        kc, qc = k_ref[rows_of[c], lanes_of[i]], q_ref[rows_of[c], lanes_of[i]]
-        own = jnp.sum(qc * kc, axis=1, keepdims=True) * strength[i, c]
-        attend[i, c] = jnp.where(diagonal, own, 0.0)
-        inverse[i, c] = jnp.where(diagonal, 1.0, 0.0)
-    for n, size in enumerate(LEVELS):
-        for i, c in pairs:
-            kc, qc = k_ref[rows_of[c], lanes_of[i]], q_ref[rows_of[c], lanes_of[i]]
-            fade = e_ref[c, n * HALF : (n + 1) * HALF, lanes_of[i]]
-            late = (row & size) != 0
-            kx = (kc * fade * jnp.where(late, 1.0, strength[i, c])).astype(BF16)
-            qx = (qc * fade).astype(BF16)
-            both = mm(jnp.concatenate([kx, qx], axis=0), kx, ((1,), (1,)))
-            mixing = jnp.where(masks[n], both[:HALF], 0.0)
-            attend[i, c] = jnp.where(masks[n], both[HALF:], attend[i, c])
-            if size == 1:
-                inverse[i, c] = inverse[i, c] - mixing
-            else:
-                own = inverse[i, c].astype(BF16)
-                inverse[i, c] = inverse[i, c] - mm(mm(own, mixing), own)
 
     def to_owner(i):
         return pltpu.make_async_remote_copy(
@@ -287,45 +293,105 @@
             device_id_type=MESH,
         )
 
-    n = len(LEVELS)
-    for i in range(heads):
-        lanes = lanes_of[i]
-        rise = [e_ref[c, n * HALF : (n + 1) * HALF, lanes] for c in range(2)]
-        fall = [e_ref[c, (n + 1) * HALF : (n + 2) * HALF, lanes] for c in range(2)]
-        whole = [part[HALF - 1 : HALF] for part in rise]
-        k = [k_ref[rows_of[c], lanes] for c in range(2)]
-        q = [q_ref[rows_of[c], lanes] for c in range(2)]
-        k_rise = [k[c] * rise[c] for c in range(2)]
-        q_rise = [q[c] * rise[c] for c in range(2)]
-        k_fall = [k[c] * fall[c] * strength[i, c] for c in range(2)]
-        cross = mm(jnp.concatenate([k_rise[1], q_rise[1]], axis=0), k_fall[0], ((1,), (1,)))
-        first = mm(
-            inverse[i, 0], jnp.concatenate([v_ref[rows_of[0], lanes], k_rise[0]], axis=1)
-        ).astype(BF16)
-        second = jnp.concatenate([v_ref[rows_of[1], lanes], k_rise[1] * whole[0]], axis=1)
-        second = mm(inverse[i, 1], second - mm(cross[:HALF], first)).astype(BF16)
-        out = [mm(attend[i, 0], first), mm(cross[HALF:], first) + mm(attend[i, 1], second)]
-        for c in range(2):
-            o_ref[rows_of[c], lanes] = out[c][:, :128]
-        r_ref[rows_of[0], lanes] = (q_rise[0] - out[0][:, 128:]).astype(BF16)
-        r_ref[rows_of[1], lanes] = (q_rise[1] * whole[0] - out[1][:, 128:]).astype(BF16)
-        stop = jnp.concatenate([k_fall[0] * whole[1], k_fall[1]], axis=0).astype(BF16)
-        maps = mm(jnp.concatenate([first, second], axis=0), stop, ((0,), (0,)))
-        move = jnp.where(diagonal, whole[0] * whole[1], 0.0) - maps[128:]
-        z_ref[i, 0:128] = move.astype(BF16)
-        z_ref[i, 128:256] = maps[:128].astype(BF16)
-
-        @pl.when(p != 2 * i)
-        def _():
-            to_owner(i).start()
-
-    def to_later(k):
+    for pair in range(0, heads, 2):
+        some = range(pair, pair + 2)
+        units = [(i, c) for i in some for c in range(2)]
+        strength, inverse = {}, {}
+        for u, (i, c) in enumerate(units):
+            kc, qc = k_ref[rows_of[c], lanes_of[i]], q_ref[rows_of[c], lanes_of[i]]
+            strength[i, c] = jnp.broadcast_to(beta[rows_of[c], i : i + 1], (HALF, 128))
+            own = jnp.sum(qc * kc, axis=1, keepdims=True) * strength[i, c]
+            attend = jnp.where(diagonal, own, 0.0)
+            for n, size in enumerate(LEVELS):
+                fade = e_ref[c, n * HALF : (n + 1) * HALF, lanes_of[i]]
+                late = (row & size) != 0
+                kx = (kc * fade * jnp.where(late, 1.0, strength[i, c])).astype(BF16)
+                qx = (qc * fade).astype(BF16)
+                both = mm(jnp.concatenate([kx, qx], axis=0), kx, ((1,), (1,)))
+                mix_ref[u, n] = jnp.where(masks[n], both[:HALF], 0.0).astype(BF16)
+                attend = jnp.where(masks[n], both[HALF:], attend)
+            attend_ref[u] = attend.astype(BF16)
+        for u, unit in enumerate(units):
+            inverse[unit] = jnp.where(diagonal, 1.0, 0.0) - mix_ref[u, 0].astype(F32)
+        for n in range(1, len(LEVELS)):
+            own = {unit: inverse[unit].astype(BF16) for unit in units}
+            left_part = {
+                unit: mm(own[unit], mix_ref[u, n]).astype(BF16) for u, unit in enumerate(units)
+            }
+            for unit in units:
+                inverse[unit] = inverse[unit] - mm(left_part[unit], own[unit])
+        inverse = {unit: inverse[unit].astype(BF16) for unit in units}
+
+        n = len(LEVELS)
+        rise = {u: e_ref[u[1], n * HALF : (n + 1) * HALF, lanes_of[u[0]]] for u in units}
+        fall = {u: e_ref[u[1], (n + 1) * HALF : (n + 2) * HALF, lanes_of[u[0]]] for u in units}
+        whole = {u: rise[u][HALF - 1 : HALF] for u in units}
+        k_rise = {u: k_ref[rows_of[u[1]], lanes_of[u[0]]] * rise[u] for u in units}
+        q_rise = {u: q_ref[rows_of[u[1]], lanes_of[u[0]]] * rise[u] for u in units}
+        k_fall = {
+            u: k_ref[rows_of[u[1]], lanes_of[u[0]]] * fall[u] * strength[u] for u in units
+        }
+        cross, first, second = {}, {}, {}
+        for i in some:
+            cross[i] = mm(
+                jnp.concatenate([k_rise[i, 1], q_rise[i, 1]], axis=0), k_fall[i, 0], ((1,), (1,))
+            ).astype(BF16)
+        for i in some:
+            first[i] = mm(
+                inverse[i, 0],
+                jnp.concatenate([v_ref[rows_of[0], lanes_of[i]], k_rise[i, 0]], axis=1),
+            ).astype(BF16)
+        late_part = {i: mm(cross[i], first[i]) for i in some}
+        for i in some:
+            start = jnp.concatenate(
+                [v_ref[rows_of[1], lanes_of[i]], k_rise[i, 1] * whole[i, 0]], axis=1
+            )
+            second[i] = mm(inverse[i, 1], start - late_part[i][:HALF]).astype(BF16)
+        for i in some:
+            stop = jnp.concatenate(
+                [k_fall[i, 0] * whole[i, 1], k_fall[i, 1]], axis=0
+            ).astype(BF16)
+            maps = mm(jnp.concatenate([first[i], second[i]], axis=0), stop, ((0,), (0,)))
+            move = jnp.where(diagonal, whole[i, 0] * whole[i, 1], 0.0) - maps[128:]
+            z_ref[i, 0:128] = move.astype(BF16)
+            z_ref[i, 128:256] = maps[:128].astype(BF16)
+
+            @pl.when(p != 2 * i)
+            def _():
+                to_owner(i).start()
+
+        for i in some:
+            lanes = lanes_of[i]
+            u = 2 * (i - pair)
+            out = [
+                mm(attend_ref[u], first[i]),
+                late_part[i][HALF:] + mm(attend_ref[u + 1], second[i]),
+            ]
+            for c in range(2):
+                o_ref[rows_of[c], lanes] = out[c][:, :128]
+            r_ref[rows_of[0], lanes] = (q_rise[i, 0] - out[0][:, 128:]).astype(BF16)
+            r_ref[rows_of[1], lanes] = (
+                q_rise[i, 1] * whole[i, 0] - out[1][:, 128:]
+            ).astype(BF16)
+
+    def to_group(k):
         return pltpu.make_async_remote_copy(
             src_ref=total,
-            dst_ref=zall.at[z],
+            dst_ref=zall.at[rank],
             send_sem=b_send.at[k],
-            recv_sem=b_recv.at[z],
-            device_id={"seq": k * PLANE + p},
+            recv_sem=b_recv.at[rank],
+            device_id={"seq": (group * GROUP + k) * PLANE + p},
+            device_id_type=MESH,
+        )
+
+    def to_next(k):
+        target = jnp.where(rank == 0, 2 * GROUP - 1 - k, GROUP + k)
+        return pltpu.make_async_remote_copy(
+            src_ref=chain.at[GROUP],
+            dst_ref=held,
+            send_sem=f_sem.at[k],
+            recv_sem=f_sem.at[2],
+            device_id={"seq": target * PLANE + p},
             device_id_type=MESH,
         )
 
@@ -339,62 +405,95 @@
             device_id_type=MESH,
         )
 
-    def send_later(k, _):
-        to_later(k).start()
-        return 0
-
-    def from_earlier(k, _):
-        pltpu.make_async_remote_copy(
-            src_ref=total,
-            dst_ref=zall.at[k],
-            send_sem=b_send.at[k],
-            recv_sem=b_recv.at[k],
-            device_id={"seq": s},
-            device_id_type=MESH,
-        ).wait_recv()
-        held[...] = (mm(held[...], zall[k, 0:128]) + zall[k, 128:256].astype(F32)).astype(BF16)
-        return 0
+    def arrived(ref, sem, k, here):
+        @pl.when(here != k)
+        def _():
+            pltpu.make_async_remote_copy(
+                src_ref=ref.at[k],
+                dst_ref=ref.at[k],
+                send_sem=sem.at[k],
+                recv_sem=sem.at[k],
+                device_id={"seq": s},
+                device_id_type=MESH,
+            ).wait_recv()
+
+    def after(so_far, ref, k):
+        step = mm(so_far, ref[k, 0:128])
+        return jnp.concatenate(
+            [step[:128].astype(BF16), (step[128:] + ref[k, 128:256].astype(F32)).astype(BF16)],
+            axis=0,
+        )
+
+    def moved(entry, at):
+        return (mm(entry, pre[at, 0:128]) + pre[at, 128:256].astype(F32)).astype(BF16)
 
     @pl.when(owner)
     def _():
         zin[p] = z_ref[y]
         for k in range(PLANE):
-
-            @pl.when(p != k)
+            arrived(zin, a_recv, k, p)
+        half_plane = PLANE // 2
+        one, two = zin[0], zin[half_plane]
+        for k in range(1, half_plane):
+            pre[k], pre[half_plane + k] = one, two
+            one, two = after(one, zin, k), after(two, zin, half_plane + k)
+        pre[half_plane] = one
+        step = mm(one, two[:128])
+        whole_map = jnp.concatenate(
+            [step[:128].astype(BF16), (step[128:] + two[128:].astype(F32)).astype(BF16)], axis=0
+        )
+        total[...] = whole_map
+        for k in range(GROUP):
+
+            @pl.when(rank != k)
             def _():
-                pltpu.make_async_remote_copy(
-                    src_ref=z_ref.at[0],
-                    dst_ref=zin.at[k],
-                    send_sem=a_send.at[0],
-                    recv_sem=a_recv.at[k],
-                    device_id={"seq": s},
-                    device_id_type=MESH,
-                ).wait_recv()
-
-            if k == 0:
-                so_far = zin[0]
+                to_group(k).start()
+
+        zall[rank] = whole_map
+        for k in range(GROUP):
+            arrived(zall, b_recv, k, rank)
+
+        @pl.when(group == 0)
+        def _():
+            chain[0] = jnp.zeros((128, 128), BF16)
+            so_far = zall[0, 128:256]
+            chain[1] = so_far
+            for k in range(1, GROUP):
+                so_far = (
+                    mm(so_far, zall[k, 0:128]) + zall[k, 128:256].astype(F32)
+                ).astype(BF16)
+                chain[k + 1] = so_far
+
+            @pl.when(feeds)
+            def _():
+                for k in range(2):
+                    to_next(k).start()
+
+            held[...] = chain[rank]
+
+        @pl.when(group == 1)
+        def _():
+            link[0, 0:128] = jnp.where(diagonal, 1.0, 0.0).astype(BF16)
+            link[0, 128:256] = jnp.zeros((128, 128), BF16)
+            so_far = zall[0]
+            link[1] = so_far
+            for k in range(1, GROUP - 1):
+                so_far = after(so_far, zall, k)
+                link[k + 1] = so_far
+            to_next(0).wait_recv()
+            held[...] = (
+                mm(held[...], link[rank, 0:128]) + link[rank, 128:256].astype(F32)
+            ).astype(BF16)
+
+        entry = held[...]
+        for q in (half_plane, 0, 1, 2, 3, 5, 6, 7):
+            if q == half_plane:
+                middle = moved(entry, q)
+                lead[q] = middle
+            elif q == 0:
+                lead[q] = entry
             else:
-                step = mm(so_far, zin[k, 0:128])
-                so_far = jnp.concatenate(
-                    [
-                        step[:128].astype(BF16),
-                        (step[128:] + zin[k, 128:256].astype(F32)).astype(BF16),
-                    ],
-                    axis=0,
-                )
-            if k < PLANE - 1:
-                pre[k + 1] = so_far
-            else:
-                total[...] = so_far
-        lax.fori_loop(z + 1, depth, send_later, 0)
-        held[...] = jnp.zeros_like(held)
-        lax.fori_loop(0, z, from_earlier, 0)
-        carry = held[...]
-        for q in range(PLANE):
-            if q == 0:
-                lead[0] = carry
-            else:
-                lead[q] = (mm(carry, pre[q, 0:128]) + pre[q, 128:256].astype(F32)).astype(BF16)
+                lead[q] = moved(entry if q < half_plane else middle, q)
 
             @pl.when(p != q)
             def _():
@@ -471,24 +570,28 @@
     for move in moves:
         move.wait_send()
 
-    @pl.when(sends_edge)
-    def _():
-        for target in range(4):
-            edge(target).wait_send()
+    for head in (0, 2, 3):
+        each_edge(head, lambda copy: copy.wait_send())
 
     for i in range(heads):
 
         @pl.when(p != 2 * i)
         def _():
             to_owner(i).wait_send()
-
-    def sent(k, _):
-        to_later(k).wait_send()
-        return 0
 
     @pl.when(owner)
     def _():
-        lax.fori_loop(z + 1, depth, sent, 0)
+        for k in range(GROUP):
+
+            @pl.when(rank != k)
+            def _():
+                to_group(k).wait_send()
+
+        @pl.when(feeds)
+        def _():
+            for k in range(2):
+                to_next(k).wait_send()
+
         for q in range(PLANE):
 
             @pl.when(p != q)
@@ -528,10 +631,14 @@
             pltpu.VMEM((count, width), BF16),
             pltpu.VMEM((count, width), F32),
             pltpu.VMEM((heads, 256, 128), BF16),
+            pltpu.VMEM((4, len(LEVELS), HALF, HALF), BF16),
+            pltpu.VMEM((4, HALF, HALF), BF16),
             pltpu.VMEM((PLANE, 256, 128), BF16),
             pltpu.VMEM((PLANE, 256, 128), BF16),
             pltpu.VMEM((256, 128), BF16),
-            pltpu.VMEM((depth, 256, 128), BF16),
+            pltpu.VMEM((GROUP, 256, 128), BF16),
+            pltpu.VMEM((GROUP + 1, 128, 128), BF16),
+            pltpu.VMEM((GROUP, 256, 128), BF16),
             pltpu.VMEM((128, 128), BF16),
             pltpu.VMEM((PLANE, 128, 128), BF16),
             pltpu.VMEM((heads, 128, 128), BF16),
@@ -539,8 +646,8 @@
             pltpu.VMEM((3, rows, model), BF16),
             pltpu.VMEM((2, rows, model), F32),
             pltpu.VMEM((3, rows, model), BF16),
-            dma((9,)), dma((6,)), dma((6,)), dma((5,)),
-            dma((heads,)), dma((PLANE,)), dma((depth,)), dma((depth,)),
+            dma((9,)), dma((6,)), dma((6,)), dma((3,)), dma((3,)),
+            dma((heads,)), dma((PLANE,)), dma((GROUP,)), dma((GROUP,)),
             dma((PLANE,)), dma((heads,)), dma((6,)), dma((6,)),
         ],
         compiler_params=pltpu.CompilerParams(

time: 67.6 us -> 61.8 us (0.914)
  Pallas kernels: 65.4 us -> 59.6 us
    pallas_call x1, Pallas kernels: 65.4 us -> 59.6 us  [layer(): pl.pallas_call(functools.partial(kernel, depth), name='layer', out_shape=...]
where the time goes in v3:
time: 61.8 us; the launch traced here: 61.3 us
  Pallas kernels  59.6 us (96%)
  local copies, waits for them, and re-layouts  1.69 us (3%)
    pallas_call x1, Pallas kernels, layer(): pl.pallas_call(functools.partial(kernel, depth), name='layer', out_shape=...  59.6 us
    unnamed x1, local copies, waits for them, and re-layouts  1.69 us

profile of v3, /device:TPU:192, one launch (start us, length us, event | category | flops | bytes accessed | tf_op | source)
XLA Modules:
  0.0 61.3 jit_solution(8232445518010967610)
XLA Ops:
  0.0 59.6 %layer.1 = bf16[64,2304]{1,0:T(8,128)(2,1)} custom-call(bf16[64,2304]{1,0:T(8,128)(2,1)} %x_hbm.1, bf16[3,2304,512]{2,1,0:T(8,128)(2,1)} %bitcast.4, bf16[2304,128]{1,0:T(8,128)(2,1)} %down_hbm.1, bf16[2304,128]{1,0:T(8,128)(2,1)} %gdown_hbm.1, bf16[4,2304]{1,0:T(4,128)(2,1)} %bitcast.5, bf16[128,512]{1,0:T(8,128)(2,1)} %up_ref.1, bf16[128,512]{1,0:T(8,128)(2,1)} %gup_ref.1, ...), custom_call_target="tpu_custom_call" | custom-call | tf_op jit(solution)/shard_map/layer/pallas_call | solution.py:610
  59.6 1.7 %copy.15 = bf16[64,2304]{1,0:T(8,128)(2,1)} copy(bf16[64,2304]{1,0:T(8,128)(2,1)} %layer.1) | data formatting | bytes 589824

commit v4 on v3

--- a/solution.py
+++ b/solution.py
@@ -47,9 +47,9 @@
     depth, x_hbm, w_hbm, down_hbm, gdown_hbm, beta_hbm, up_ref, gup_ref, conv_ref, dlog_ref,
     bias_ref, span_hbm, gain_ref, ow_hbm, out_ref,
     x_ref, w_ref, dg_ref, beta_ref, span_ref, ow_ref,
-    proj_ref, low_ref, strength_ref, q_ref, k_ref, v_ref, e_ref, o_ref, r_ref, gate_ref, z_ref,
-    mix_ref, attend_ref, zin, pre, total, zall, chain, link, held, lead, state, normed, part, sums, inbox,
-    l_sem, x_send, x_recv, e_sem, f_sem,
+    proj_ref, fade_ref, strength_ref, q_ref, k_ref, v_ref, e_ref, o_ref, r_ref, gate_ref, z_ref,
+    mix_ref, attend_ref, zin, pre, total, zall, chain, link, held, entry, lead, state, normed, part, sums, inbox,
+    l_sem, x_send, x_recv, e_sem, f_sem, g_send, g_recv,
     a_send, a_recv, b_send, b_recv, c_send, c_recv, d_send, d_recv,
 ):
     s = lax.axis_index("seq")
@@ -185,8 +185,10 @@
 
     each_edge(3, lambda copy: copy.start())
     moves[0].wait_recv()
+    moves[2].wait_send()
     moves[4].start()
     moves[1].wait_recv()
+    moves[3].wait_send()
     moves[5].start()
     each_edge(2, lambda copy: copy.start())
     for load in loads[:7]:
@@ -194,6 +196,10 @@
     moves[2].wait_recv()
     each_edge(0, lambda copy: copy.start())
     moves[3].wait_recv()
+
+    rate = jnp.concatenate(
+        [jnp.exp(jnp.full((1, 128), dlog_ref[i], F32)) for i in range(heads)], axis=1
+    )
 
     def project(first, slots):
         size = len(slots) * rows
@@ -205,9 +211,15 @@
                 some, beta_ref[...], (((1,), (1,)), ((), ())), preferred_element_type=F32
             )
         )
+        raw = jnp.dot(both[:, 0:128], up_ref[...], preferred_element_type=F32) + bias_ref[...]
+        soft = jnp.maximum(raw, 0.0) + jnp.log1p(jnp.exp(-jnp.abs(raw)))
+        log_decay = -rate * soft
+        gate = sigmoid(jnp.dot(both[:, 128:256], gup_ref[...], preferred_element_type=F32))
         for n, where in enumerate(at):
-            low_ref[where, :] = both[n * rows : (n + 1) * rows]
-            strength_ref[where, :] = force[n * rows : (n + 1) * rows]
+            own = slice(n * rows, (n + 1) * rows)
+            fade_ref[where, :] = log_decay[own]
+            gate_ref[where, :] = gate[own]
+            strength_ref[where, :] = force[own]
 
     def project_qkv(c, first, slots, tail):
         size = len(slots) * rows
@@ -234,15 +246,9 @@
     for c in range(3):
         project_qkv(c, 3 * rows, (far,), HALO)
 
-    raw = jnp.dot(low_ref[:, 0:128], up_ref[...], preferred_element_type=F32) + bias_ref[...]
-    soft = jnp.maximum(raw, 0.0) + jnp.log1p(jnp.exp(-jnp.abs(raw)))
-    rate = jnp.concatenate(
-        [jnp.exp(jnp.full((1, 128), dlog_ref[i], F32)) for i in range(heads)], axis=1
-    )
-    log_decay = -rate * soft
     loads[7].wait()
     for c in range(2):
-        piece_of = log_decay[c * HALF : (c + 1) * HALF]
+        piece_of = fade_ref[c * HALF : (c + 1) * HALF, :]
         top = piece_of.astype(BF16)
         rest = (piece_of - top.astype(F32)).astype(BF16)
         e_ref[c] = jnp.exp(
@@ -250,9 +256,6 @@
                 span_ref[...], jnp.concatenate([top, rest], axis=0), preferred_element_type=F32
             )
         )
-    gate_ref[...] = sigmoid(
-        jnp.dot(low_ref[:, 128:256], gup_ref[...], preferred_element_type=F32)
-    )
     beta = strength_ref[...]
 
     for c, target in enumerate((q_ref, k_ref, v_ref)):
@@ -374,20 +377,30 @@
                 q_rise[i, 1] * whole[i, 0] - out[1][:, 128:]
             ).astype(BF16)
 
-    def to_group(k):
-        return pltpu.make_async_remote_copy(
-            src_ref=total,
-            dst_ref=zall.at[rank],
+    def to_group(k, at):
+        return pltpu.make_async_remote_copy(
+            src_ref=total.at[at],
+            dst_ref=zall.at[rank, at],
             send_sem=b_send.at[k],
             recv_sem=b_recv.at[rank],
             device_id={"seq": (group * GROUP + k) * PLANE + p},
             device_id_type=MESH,
         )
 
+    def from_group(k, at):
+        return pltpu.make_async_remote_copy(
+            src_ref=total.at[at],
+            dst_ref=zall.at[k, at],
+            send_sem=b_send.at[k],
+            recv_sem=b_recv.at[k],
+            device_id={"seq": s},
+            device_id_type=MESH,
+        )
+
     def to_next(k):
         target = jnp.where(rank == 0, 2 * GROUP - 1 - k, GROUP + k)
         return pltpu.make_async_remote_copy(
-            src_ref=chain.at[GROUP],
+            src_ref=chain,
             dst_ref=held,
             send_sem=f_sem.at[k],
             recv_sem=f_sem.at[2],
@@ -395,9 +408,19 @@
             device_id_type=MESH,
         )
 
-    def to_block(q):
-        return pltpu.make_async_remote_copy(
-            src_ref=lead.at[q],
+    def prefix_to(q):
+        return pltpu.make_async_remote_copy(
+            src_ref=pre.at[q],
+            dst_ref=lead.at[y],
+            send_sem=g_send.at[q],
+            recv_sem=g_recv.at[y],
+            device_id={"seq": base + q},
+            device_id_type=MESH,
+        )
+
+    def entry_to(q):
+        return pltpu.make_async_remote_copy(
+            src_ref=entry,
             dst_ref=state.at[y],
             send_sem=c_send.at[q],
             recv_sem=c_recv.at[y],
@@ -405,113 +428,159 @@
             device_id_type=MESH,
         )
 
-    def arrived(ref, sem, k, here):
-        @pl.when(here != k)
-        def _():
-            pltpu.make_async_remote_copy(
-                src_ref=ref.at[k],
-                dst_ref=ref.at[k],
-                send_sem=sem.at[k],
-                recv_sem=sem.at[k],
-                device_id={"seq": s},
-                device_id_type=MESH,
-            ).wait_recv()
-
-    def after(so_far, ref, k):
-        step = mm(so_far, ref[k, 0:128])
+    def landed(ref, sem, k):
+        pltpu.make_async_remote_copy(
+            src_ref=ref.at[k],
+            dst_ref=ref.at[k],
+            send_sem=sem.at[k],
+            recv_sem=sem.at[k],
+            device_id={"seq": s},
+            device_id_type=MESH,
+        ).wait_recv()
+
+    everything, shift_only = pl.ds(0, 256), pl.ds(128, 128)
+    half_plane = PLANE // 2
+
+    def join(one, two):
+        step = mm(one, two[:128])
         return jnp.concatenate(
-            [step[:128].astype(BF16), (step[128:] + ref[k, 128:256].astype(F32)).astype(BF16)],
-            axis=0,
-        )
-
-    def moved(entry, at):
-        return (mm(entry, pre[at, 0:128]) + pre[at, 128:256].astype(F32)).astype(BF16)
+            [step[:128].astype(BF16), (step[128:] + two[128:].astype(F32)).astype(BF16)], axis=0
+        )
+
+    def moved(state_in, both):
+        return (mm(state_in, both[0:128]) + both[128:256].astype(F32)).astype(BF16)
+
+    def group_copies(act):
+        for k in range(GROUP):
+            @pl.when(jnp.logical_and(jnp.logical_and(group == 0, rank == 0), k > 0))
+            def _():
+                act(to_group(k, shift_only))
+
+            wanted = k > rank
+            if k == 0:
+                wanted = jnp.logical_and(group == 0, rank > 0)
+            else:
+                wanted = jnp.logical_and(
+                    wanted, jnp.logical_or(group == 1, rank > 0)
+                )
+
+            @pl.when(wanted)
+            def _():
+                act(to_group(k, everything))
 
     @pl.when(owner)
     def _():
         zin[p] = z_ref[y]
         for k in range(PLANE):
-            arrived(zin, a_recv, k, p)
-        half_plane = PLANE // 2
+
+            @pl.when(p != k)
+            def _():
+                landed(zin, a_recv, k)
+
         one, two = zin[0], zin[half_plane]
+        later = {}
         for k in range(1, half_plane):
-            pre[k], pre[half_plane + k] = one, two
-            one, two = after(one, zin, k), after(two, zin, half_plane + k)
+            pre[k], later[half_plane + k] = one, two
+            one, two = join(one, zin[k]), join(two, zin[half_plane + k])
         pre[half_plane] = one
-        step = mm(one, two[:128])
-        whole_map = jnp.concatenate(
-            [step[:128].astype(BF16), (step[128:] + two[128:].astype(F32)).astype(BF16)], axis=0
-        )
+        whole_map = join(one, two)
         total[...] = whole_map
-        for k in range(GROUP):
-
-            @pl.when(rank != k)
-            def _():
-                to_group(k).start()
-
+        group_copies(lambda copy: copy.start())
         zall[rank] = whole_map
-        for k in range(GROUP):
-            arrived(zall, b_recv, k, rank)
+        for k in range(half_plane + 1, PLANE):
+            pre[k] = join(one, later[k])
+        for q in range(1, PLANE):
+
+            @pl.when(p != q)
+            def _():
+                prefix_to(q).start()
+
+        @pl.when(p > 0)
+        def _():
+            lead[y] = pre[p]
 
         @pl.when(group == 0)
         def _():
-            chain[0] = jnp.zeros((128, 128), BF16)
-            so_far = zall[0, 128:256]
-            chain[1] = so_far
-            for k in range(1, GROUP):
-                so_far = (
-                    mm(so_far, zall[k, 0:128]) + zall[k, 128:256].astype(F32)
-                ).astype(BF16)
-                chain[k + 1] = so_far
+            chain[...] = jnp.zeros_like(chain)
+            entry[...] = jnp.zeros_like(entry)
+            for k in range(GROUP):
+                needed = jnp.logical_or(feeds, k < rank)
+                if k == 0:
+
+                    @pl.when(rank > 0)
+                    def _():
+                        from_group(0, shift_only).wait_recv()
+
+                else:
+
+                    @pl.when(jnp.logical_and(needed, rank != k))
+                    def _():
+                        from_group(k, everything).wait_recv()
+
+                @pl.when(rank == k)
+                def _():
+                    entry[...] = chain[...]
+
+                @pl.when(needed)
+                def _():
+                    if k == 0:
+                        chain[...] = zall[0, 128:256]
+                    else:
+                        chain[...] = moved(chain[...], zall[k])
 
             @pl.when(feeds)
             def _():
                 for k in range(2):
                     to_next(k).start()
 
-            held[...] = chain[rank]
-
         @pl.when(group == 1)
         def _():
-            link[0, 0:128] = jnp.where(diagonal, 1.0, 0.0).astype(BF16)
-            link[0, 128:256] = jnp.zeros((128, 128), BF16)
-            so_far = zall[0]
-            link[1] = so_far
-            for k in range(1, GROUP - 1):
-                so_far = after(so_far, zall, k)
-                link[k + 1] = so_far
+            for k in range(GROUP - 1):
+
+                @pl.when(k < rank)
+                def _():
+                    from_group(k, everything).wait_recv()
+                    if k == 0:
+                        link[...] = zall[0]
+                    else:
+                        link[...] = join(link[...], zall[k])
+
             to_next(0).wait_recv()
-            held[...] = (
-                mm(held[...], link[rank, 0:128]) + link[rank, 128:256].astype(F32)
-            ).astype(BF16)
-
-        entry = held[...]
-        for q in (half_plane, 0, 1, 2, 3, 5, 6, 7):
-            if q == half_plane:
-                middle = moved(entry, q)
-                lead[q] = middle
-            elif q == 0:
-                lead[q] = entry
-            else:
-                lead[q] = moved(entry if q < half_plane else middle, q)
+
+            @pl.when(rank == 0)
+            def _():
+                entry[...] = held[...]
+
+            @pl.when(rank > 0)
+            def _():
+                entry[...] = moved(held[...], link[...])
+
+        for q in range(PLANE):
 
             @pl.when(p != q)
             def _():
-                to_block(q).start()
-
-        state[y] = lead[p]
+                entry_to(q).start()
+
+        state[y] = entry[...]
+
+    @pl.when(p > 0)
+    def _():
+        for i in range(heads):
+
+            @pl.when(p != 2 * i)
+            def _():
+                landed(lead, g_recv, i)
+
+        for i in range(heads):
+            lanes = lanes_of[i]
+            both = mm(r_ref[:, lanes], lead[i], ((1,), (1,)))
+            o_ref[:, lanes] = o_ref[:, lanes] + both[:, 128:]
+            r_ref[:, lanes] = both[:, :128].astype(BF16)
 
     def states_in(i):
         @pl.when(p != 2 * i)
         def _():
-            pltpu.make_async_remote_copy(
-                src_ref=lead.at[0],
-                dst_ref=state.at[i],
-                send_sem=c_send.at[0],
-                recv_sem=c_recv.at[i],
-                device_id={"seq": s},
-                device_id_type=MESH,
-            ).wait_recv()
+            landed(state, c_recv, i)
 
     for i in range(heads):
         states_in(i)
@@ -567,8 +636,8 @@
 
     for copy in (far_right, far_left, right_low, left_top, right_top, left_low):
         copy.wait_send()
-    for move in moves:
-        move.wait_send()
+    for n in (0, 1, 4, 5):
+        moves[n].wait_send()
 
     for head in (0, 2, 3):
         each_edge(head, lambda copy: copy.wait_send())
@@ -581,11 +650,7 @@
 
     @pl.when(owner)
     def _():
-        for k in range(GROUP):
-
-            @pl.when(rank != k)
-            def _():
-                to_group(k).wait_send()
+        group_copies(lambda copy: copy.wait_send())
 
         @pl.when(feeds)
         def _():
@@ -596,7 +661,9 @@
 
             @pl.when(p != q)
             def _():
-                to_block(q).wait_send()
+                if q > 0:
+                    prefix_to(q).wait_send()
+                entry_to(q).wait_send()
 
 
 def layer(depth, x, w, down, gdown, beta, up, gup, conv, dlog, bias, span, gain, ow):
@@ -621,7 +688,7 @@
             pltpu.VMEM(span.shape, BF16),
             pltpu.VMEM(ow.shape, BF16),
             pltpu.VMEM((3, HALO + count, width), F32),
-            pltpu.VMEM((count, 256), BF16),
+            pltpu.VMEM((count, width), F32),
             pltpu.VMEM((count, heads), F32),
             pltpu.VMEM((count, width), F32),
             pltpu.VMEM((count, width), F32),
@@ -637,16 +704,17 @@
             pltpu.VMEM((PLANE, 256, 128), BF16),
             pltpu.VMEM((256, 128), BF16),
             pltpu.VMEM((GROUP, 256, 128), BF16),
-            pltpu.VMEM((GROUP + 1, 128, 128), BF16),
-            pltpu.VMEM((GROUP, 256, 128), BF16),
             pltpu.VMEM((128, 128), BF16),
-            pltpu.VMEM((PLANE, 128, 128), BF16),
+            pltpu.VMEM((256, 128), BF16),
+            pltpu.VMEM((128, 128), BF16),
+            pltpu.VMEM((128, 128), BF16),
+            pltpu.VMEM((heads, 256, 128), BF16),
             pltpu.VMEM((heads, 128, 128), BF16),
             pltpu.VMEM((count, width), BF16),
             pltpu.VMEM((3, rows, model), BF16),
             pltpu.VMEM((2, rows, model), F32),
             pltpu.VMEM((3, rows, model), BF16),
-            dma((9,)), dma((6,)), dma((6,)), dma((3,)), dma((3,)),
+            dma((9,)), dma((6,)), dma((6,)), dma((3,)), dma((3,)), dma((PLANE,)), dma((heads,)),
             dma((heads,)), dma((PLANE,)), dma((GROUP,)), dma((GROUP,)),
             dma((PLANE,)), dma((heads,)), dma((6,)), dma((6,)),
         ],

time: 61.8 us -> 61.2 us (level)
  no operation moved by 1% of the time
where the time goes in v4:
time: 61.2 us; the launch traced here: 60.8 us
  Pallas kernels  59.1 us (97%)
  local copies, waits for them, and re-layouts  1.69 us (3%)
    pallas_call x1, Pallas kernels, layer(): pl.pallas_call(functools.partial(kernel, depth), name='layer', out_shape=...  59.1 us
    unnamed x1, local copies, waits for them, and re-layouts  1.69 us

profile of v4, /device:TPU:192, one launch (start us, length us, event | category | flops | bytes accessed | tf_op | source)
XLA Modules:
  0.0 60.8 jit_solution(9073247181864461414)
XLA Ops:
  0.0 59.1 %layer.1 = bf16[64,2304]{1,0:T(8,128)(2,1)} custom-call(bf16[64,2304]{1,0:T(8,128)(2,1)} %x_hbm.1, bf16[3,2304,512]{2,1,0:T(8,128)(2,1)} %bitcast.4, bf16[2304,128]{1,0:T(8,128)(2,1)} %down_hbm.1, bf16[2304,128]{1,0:T(8,128)(2,1)} %gdown_hbm.1, bf16[4,2304]{1,0:T(4,128)(2,1)} %bitcast.5, bf16[128,512]{1,0:T(8,128)(2,1)} %up_ref.1, bf16[128,512]{1,0:T(8,128)(2,1)} %gup_ref.1, ...), custom_call_target="tpu_custom_call" | custom-call | tf_op jit(solution)/shard_map/layer/pallas_call | solution.py:677
  59.1 1.7 %copy.15 = bf16[64,2304]{1,0:T(8,128)(2,1)} copy(bf16[64,2304]{1,0:T(8,128)(2,1)} %layer.1) | data formatting | bytes 589824

commit v5 on v4

--- a/solution.py
+++ b/solution.py
@@ -18,6 +18,8 @@
 LEVELS = (1, 2, 4, 8, 16, 32, 64)
 PLANE = 8
 GROUP = 4
+FAR_FIRST = (4, 5, 2, 3, 6, 7, 1)
+ENTRIES = (7, 4, 2, 3, 6, 1)
 
 
 def span_matrix():
@@ -44,9 +46,10 @@
 
 
 def kernel(
-    depth, x_hbm, w_hbm, down_hbm, gdown_hbm, beta_hbm, up_ref, gup_ref, conv_ref, dlog_ref,
-    bias_ref, span_hbm, gain_ref, ow_hbm, out_ref,
-    x_ref, w_ref, dg_ref, beta_ref, span_ref, ow_ref,
+    depth, x_hbm, w_hbm, down_hbm, gdown_hbm, beta_hbm, up_hbm, gup_hbm, conv_hbm, dlog_hbm,
+    bias_hbm, span_hbm, gain_hbm, ow_hbm, out_ref,
+    x_ref, w_ref, dg_ref, beta_ref, up_ref, gup_ref, conv_ref, dlog_ref, bias_ref, span_ref,
+    gain_ref, ow_ref,
     proj_ref, fade_ref, strength_ref, q_ref, k_ref, v_ref, e_ref, o_ref, r_ref, gate_ref, z_ref,
     mix_ref, attend_ref, zin, pre, total, zall, chain, link, held, entry, lead, state, normed, part, sums, inbox,
     l_sem, x_send, x_recv, e_sem, f_sem, g_send, g_recv,
@@ -63,7 +66,7 @@
     group, rank = lax.div(z, GROUP), lax.rem(z, GROUP)
     feeds = jnp.logical_and(group == 0, jnp.logical_or(rank == 0, rank == GROUP - 1))
     has_next = s < depth * PLANE - 1
-    edge_from = jnp.where(h == 1, 3, h)
+    edge_from = jnp.where(h == 1, 2, h)
     rows = x_hbm.shape[0]
     half = rows // 2
     count = 4 * rows
@@ -87,6 +90,12 @@
         def _():
             pl.semaphore_signal(barrier, 1, device_id={"seq": base + q}, device_id_type=MESH)
 
+    @pl.when(core == 1)
+    def _():
+        pl.semaphore_signal(
+            barrier, 1, device_id={"seq": base + lax.rem(p + 2, PLANE)}, device_id_type=MESH
+        )
+
     @pl.when(owner)
     def _():
         for d in range(1, GROUP):
@@ -104,9 +113,9 @@
 
     greeted = (
         2
-        + jnp.where(owner, PLANE - 1 + GROUP - 1, PLANE // 2)
+        + jnp.where(owner, PLANE - 1 + GROUP - 1, PLANE // 2 + 1)
         + jnp.where(jnp.logical_and(owner, feeds), 2, 0)
-        + jnp.where(has_next, jnp.where(h == 3, 2, jnp.where(h == 1, 0, 1)), 0)
+        + jnp.where(has_next, jnp.where(h == 2, 2, jnp.where(h == 1, 0, 1)), 0)
     )
 
     loads = [
@@ -120,6 +129,12 @@
                 (down_hbm, dg_ref.at[:, pl.ds(0, 128)]),
                 (gdown_hbm, dg_ref.at[:, pl.ds(128, 128)]),
                 (beta_hbm, beta_ref),
+                (up_hbm, up_ref),
+                (gup_hbm, gup_ref),
+                (conv_hbm, conv_ref),
+                (dlog_hbm, dlog_ref),
+                (bias_hbm, bias_ref),
+                (gain_hbm, gain_ref),
                 (span_hbm, span_ref),
                 (ow_hbm, ow_ref),
             ]
@@ -148,7 +163,8 @@
     def rows_at(slot, half_at):
         return x_ref.at[pl.ds(slot * rows + half_at * half, half)]
 
-    mine = [x_hbm.at[pl.ds(0, half)], x_hbm.at[pl.ds(half, half)]]
+    loads[0].wait()
+    mine = [rows_at(0, 0), rows_at(0, 1)]
     moves = [
         piece(mine[0], 1, 0, right, 0),
         piece(mine[1], 2, 1, left, 1),
@@ -172,9 +188,12 @@
 
     last = pl.ds(rows - EDGE, EDGE)
     edges = {
-        3: [edge(0, x_hbm.at[last], 3), edge(1, x_hbm.at[last], 1)],
+        3: [edge(0, x_ref.at[last], 3)],
         0: [edge(0, x_ref.at[pl.ds(2 * rows - EDGE, EDGE)], 0)],
-        2: [edge(0, x_ref.at[pl.ds(3 * rows - EDGE, EDGE)], 2)],
+        2: [
+            edge(0, x_ref.at[pl.ds(3 * rows - EDGE, EDGE)], 2),
+            edge(1, x_ref.at[pl.ds(3 * rows - EDGE, EDGE)], 1),
+        ],
     }
 
     def each_edge(head, act):
@@ -191,7 +210,7 @@
     moves[3].wait_send()
     moves[5].start()
     each_edge(2, lambda copy: copy.start())
-    for load in loads[:7]:
+    for load in loads[1:14]:
         load.wait()
     moves[2].wait_recv()
     each_edge(0, lambda copy: copy.start())
@@ -242,12 +261,7 @@
     def _():
         edges[0][0].wait_recv()
 
-    project(3 * rows, (far,))
-    for c in range(3):
-        project_qkv(c, 3 * rows, (far,), HALO)
-
-    loads[7].wait()
-    for c in range(2):
+    def decays(c):
         piece_of = fade_ref[c * HALF : (c + 1) * HALF, :]
         top = piece_of.astype(BF16)
         rest = (piece_of - top.astype(F32)).astype(BF16)
@@ -256,9 +270,9 @@
                 span_ref[...], jnp.concatenate([top, rest], axis=0), preferred_element_type=F32
             )
         )
-    beta = strength_ref[...]
-
-    for c, target in enumerate((q_ref, k_ref, v_ref)):
+
+    def convolve(c):
+        target = (q_ref, k_ref, v_ref)[c]
         taps = conv_ref[c].astype(F32)
         mixed = proj_ref[c, pl.ds(HALO - 3, count), :] * taps[0:1]
         for i in range(1, 4):
@@ -266,7 +280,7 @@
         mixed = (mixed * sigmoid(mixed)).astype(BF16).astype(F32)
         if c == 2:
             target[...] = mixed
-            continue
+            return
         for i in range(heads):
             lanes = slice(i * 128, (i + 1) * 128)
             u = mixed[:, lanes]
@@ -275,6 +289,17 @@
                 scale = scale * (128**-0.5)
             target[:, lanes] = u * scale
 
+    project(3 * rows, (far,))
+    project_qkv(1, 3 * rows, (far,), HALO)
+    decays(0)
+    project_qkv(0, 3 * rows, (far,), HALO)
+    convolve(1)
+    decays(1)
+    project_qkv(2, 3 * rows, (far,), HALO)
+    convolve(0)
+    convolve(2)
+    beta = strength_ref[...]
+
     t = lax.broadcasted_iota(jnp.int32, (HALF, HALF), 0)
     j = lax.broadcasted_iota(jnp.int32, (HALF, HALF), 1)
     row = lax.broadcasted_iota(jnp.int32, (HALF, 128), 0)
@@ -296,36 +321,58 @@
             device_id_type=MESH,
         )
 
-    for pair in range(0, heads, 2):
-        some = range(pair, pair + 2)
-        units = [(i, c) for i in some for c in range(2)]
-        strength, inverse = {}, {}
-        for u, (i, c) in enumerate(units):
-            kc, qc = k_ref[rows_of[c], lanes_of[i]], q_ref[rows_of[c], lanes_of[i]]
+    strength, inverse = {}, {}
+
+    def unit_of(i, c):
+        return 2 * i + c
+
+    def mix(i, c, n, attend):
+        kc, qc = k_ref[rows_of[c], lanes_of[i]], q_ref[rows_of[c], lanes_of[i]]
+        if n == 0:
             strength[i, c] = jnp.broadcast_to(beta[rows_of[c], i : i + 1], (HALF, 128))
             own = jnp.sum(qc * kc, axis=1, keepdims=True) * strength[i, c]
             attend = jnp.where(diagonal, own, 0.0)
-            for n, size in enumerate(LEVELS):
-                fade = e_ref[c, n * HALF : (n + 1) * HALF, lanes_of[i]]
-                late = (row & size) != 0
-                kx = (kc * fade * jnp.where(late, 1.0, strength[i, c])).astype(BF16)
-                qx = (qc * fade).astype(BF16)
-                both = mm(jnp.concatenate([kx, qx], axis=0), kx, ((1,), (1,)))
-                mix_ref[u, n] = jnp.where(masks[n], both[:HALF], 0.0).astype(BF16)
-                attend = jnp.where(masks[n], both[HALF:], attend)
-            attend_ref[u] = attend.astype(BF16)
-        for u, unit in enumerate(units):
-            inverse[unit] = jnp.where(diagonal, 1.0, 0.0) - mix_ref[u, 0].astype(F32)
+        size = LEVELS[n]
+        fade = e_ref[c, n * HALF : (n + 1) * HALF, lanes_of[i]]
+        late = (row & size) != 0
+        kx = (kc * fade * jnp.where(late, 1.0, strength[i, c])).astype(BF16)
+        qx = (qc * fade).astype(BF16)
+        both = mm(jnp.concatenate([kx, qx], axis=0), kx, ((1,), (1,)))
+        mix_ref[unit_of(i, c), n] = jnp.where(masks[n], both[:HALF], 0.0).astype(BF16)
+        attend = jnp.where(masks[n], both[HALF:], attend)
+        if n == len(LEVELS) - 1:
+            attend_ref[unit_of(i, c)] = attend.astype(BF16)
+        return attend
+
+    def mixes(some):
+        for i in some:
+            for c in range(2):
+                attend = None
+                for n in range(len(LEVELS)):
+                    attend = mix(i, c, n, attend)
+                    yield
+
+    def doublings(some):
+        units = [(i, c) for i in some for c in range(2)]
+        for unit in units:
+            inverse[unit] = jnp.where(diagonal, 1.0, 0.0) - mix_ref[unit_of(*unit), 0].astype(F32)
         for n in range(1, len(LEVELS)):
             own = {unit: inverse[unit].astype(BF16) for unit in units}
-            left_part = {
-                unit: mm(own[unit], mix_ref[u, n]).astype(BF16) for u, unit in enumerate(units)
-            }
+            left_part = {}
+            for unit in units:
+                left_part[unit] = mm(own[unit], mix_ref[unit_of(*unit), n]).astype(BF16)
+            yield
             for unit in units:
                 inverse[unit] = inverse[unit] - mm(left_part[unit], own[unit])
-        inverse = {unit: inverse[unit].astype(BF16) for unit in units}
-
+            yield
+        for unit in units:
+            inverse[unit] = inverse[unit].astype(BF16)
+
+    parts = {}
+
+    def maps_of(some):
         n = len(LEVELS)
+        units = [(i, c) for i in some for c in range(2)]
         rise = {u: e_ref[u[1], n * HALF : (n + 1) * HALF, lanes_of[u[0]]] for u in units}
         fall = {u: e_ref[u[1], (n + 1) * HALF : (n + 2) * HALF, lanes_of[u[0]]] for u in units}
         whole = {u: rise[u][HALF - 1 : HALF] for u in units}
@@ -344,12 +391,15 @@
                 inverse[i, 0],
                 jnp.concatenate([v_ref[rows_of[0], lanes_of[i]], k_rise[i, 0]], axis=1),
             ).astype(BF16)
+        yield
         late_part = {i: mm(cross[i], first[i]) for i in some}
+        yield
         for i in some:
             start = jnp.concatenate(
                 [v_ref[rows_of[1], lanes_of[i]], k_rise[i, 1] * whole[i, 0]], axis=1
             )
             second[i] = mm(inverse[i, 1], start - late_part[i][:HALF]).astype(BF16)
+        yield
         for i in some:
             stop = jnp.concatenate(
                 [k_fall[i, 0] * whole[i, 1], k_fall[i, 1]], axis=0
@@ -358,17 +408,15 @@
             move = jnp.where(diagonal, whole[i, 0] * whole[i, 1], 0.0) - maps[128:]
             z_ref[i, 0:128] = move.astype(BF16)
             z_ref[i, 128:256] = maps[:128].astype(BF16)
-
-            @pl.when(p != 2 * i)
-            def _():
-                to_owner(i).start()
-
+            parts[i] = (q_rise, whole, first, second, late_part)
+
+    def outputs_of(some):
         for i in some:
+            q_rise, whole, first, second, late_part = parts[i]
             lanes = lanes_of[i]
-            u = 2 * (i - pair)
             out = [
-                mm(attend_ref[u], first[i]),
-                late_part[i][HALF:] + mm(attend_ref[u + 1], second[i]),
+                mm(attend_ref[unit_of(i, 0)], first[i]),
+                late_part[i][HALF:] + mm(attend_ref[unit_of(i, 1)], second[i]),
             ]
             for c in range(2):
                 o_ref[rows_of[c], lanes] = out[c][:, :128]
@@ -376,6 +424,38 @@
             r_ref[rows_of[1], lanes] = (
                 q_rise[i, 1] * whole[i, 0] - out[1][:, 128:]
             ).astype(BF16)
+            yield
+
+    def send_maps(some):
+        for i in some:
+
+            @pl.when(p != 2 * i)
+            def _():
+                to_owner(i).start()
+
+    def together(main, other, share):
+        for _ in main:
+            for _ in range(share):
+                next(other, None)
+
+    def finish(*works):
+        for work in works:
+            for _ in work:
+                pass
+
+    early, late_heads = range(0, heads, 2), range(1, heads, 2)
+    finish(mixes(early))
+    other = mixes(late_heads)
+    together(doublings(early), other, 3)
+    finish(other)
+    other = doublings(late_heads)
+    together(maps_of(early), other, 1)
+    send_maps(early)
+    outputs = outputs_of(early)
+    together(other, outputs, 1)
+    finish(outputs, maps_of(late_heads))
+    send_maps(late_heads)
+    finish(outputs_of(late_heads))
 
     def to_group(k, at):
         return pltpu.make_async_remote_copy(
@@ -489,9 +569,10 @@
         zall[rank] = whole_map
         for k in range(half_plane + 1, PLANE):
             pre[k] = join(one, later[k])
-        for q in range(1, PLANE):
-
-            @pl.when(p != q)
+        for d in FAR_FIRST:
+            q = lax.rem(p + d, PLANE)
+
+            @pl.when(q > 0)
             def _():
                 prefix_to(q).start()
 
@@ -555,13 +636,16 @@
             def _():
                 entry[...] = moved(held[...], link[...])
 
-        for q in range(PLANE):
-
-            @pl.when(p != q)
-            def _():
-                entry_to(q).start()
-
-        state[y] = entry[...]
+        @pl.when(z > 0)
+        def _():
+            for d in ENTRIES:
+                entry_to(lax.rem(p + d, PLANE)).start()
+
+            state[y] = entry[...]
+
+    @pl.when(z == 0)
+    def _():
+        state[...] = jnp.zeros_like(state)
 
     @pl.when(p > 0)
     def _():
@@ -577,18 +661,34 @@
             o_ref[:, lanes] = o_ref[:, lanes] + both[:, 128:]
             r_ref[:, lanes] = both[:, :128].astype(BF16)
 
-    def states_in(i):
-        @pl.when(p != 2 * i)
+    after_own = lax.rem(y + 1, heads)
+    passes_on = jnp.logical_and(core == 1, z > 0)
+    passed = pltpu.make_async_remote_copy(
+        src_ref=state.at[after_own],
+        dst_ref=state.at[after_own],
+        send_sem=c_send.at[0],
+        recv_sem=c_recv.at[after_own],
+        device_id={"seq": base + lax.rem(p + PLANE - 2, PLANE)},
+        device_id_type=MESH,
+    )
+    for d in (1, 0, 3, 2):
+        i = lax.rem(y + d, heads)
+
+        @pl.when(jnp.logical_and(p != 2 * i, z > 0))
         def _():
             landed(state, c_recv, i)
 
-    for i in range(heads):
-        states_in(i)
-        lanes = lanes_of[i]
+        if d == 1:
+
+            @pl.when(passes_on)
+            def _():
+                passed.start()
+
+        lanes = pl.ds(pl.multiple_of(i * 128, 128), 128)
         attended = o_ref[:, lanes] + mm(r_ref[:, lanes], state[i], ((1,), (1,)))
         scale = lax.rsqrt(jnp.mean(attended * attended, axis=1, keepdims=True) + 1e-05)
         normed[:, lanes] = (attended * scale * gain_ref[...] * gate_ref[:, lanes]).astype(BF16)
-    loads[8].wait()
+    loads[14].wait()
 
 
     def partial(to):
@@ -657,18 +757,25 @@
             for k in range(2):
                 to_next(k).wait_send()
 
-        for q in range(PLANE):
-
-            @pl.when(p != q)
-            def _():
-                if q > 0:
-                    prefix_to(q).wait_send()
-                entry_to(q).wait_send()
+        for d in FAR_FIRST:
+            q = lax.rem(p + d, PLANE)
+
+            @pl.when(q > 0)
+            def _():
+                prefix_to(q).wait_send()
+
+        @pl.when(z > 0)
+        def _():
+            for d in ENTRIES:
+                entry_to(lax.rem(p + d, PLANE)).wait_send()
+
+    @pl.when(passes_on)
+    def _():
+        passed.wait_send()
 
 
 def layer(depth, x, w, down, gdown, beta, up, gup, conv, dlog, bias, span, gain, ow):
     vmem = pl.BlockSpec(memory_space=pltpu.VMEM)
-    smem = pl.BlockSpec(memory_space=pltpu.SMEM)
     hbm = pl.BlockSpec(memory_space=pl.ANY)
     rows, model = x.shape
     count, width = 4 * rows, w.shape[2]
@@ -677,15 +784,21 @@
     return pl.pallas_call(
         functools.partial(kernel, depth),
         name="layer",
-        out_shape=jax.ShapeDtypeStruct((rows, model), BF16),
-        in_specs=[hbm] * 5 + [vmem] * 3 + [smem, vmem, hbm, vmem, hbm],
+        out_shape=pltpu.VMEM((rows, model), BF16),
+        in_specs=[hbm] * 13,
         out_specs=vmem,
         scratch_shapes=[
             pltpu.VMEM((count + HALO, model), BF16),
             pltpu.VMEM(w.shape, BF16),
             pltpu.VMEM((model, 256), BF16),
             pltpu.VMEM(beta.shape, BF16),
+            pltpu.VMEM(up.shape, BF16),
+            pltpu.VMEM(gup.shape, BF16),
+            pltpu.VMEM(conv.shape, BF16),
+            pltpu.SMEM(dlog.shape, F32),
+            pltpu.VMEM(bias.shape, F32),
             pltpu.VMEM(span.shape, BF16),
+            pltpu.VMEM(gain.shape, F32),
             pltpu.VMEM(ow.shape, BF16),
             pltpu.VMEM((3, HALO + count, width), F32),
             pltpu.VMEM((count, width), F32),
@@ -698,8 +811,8 @@
             pltpu.VMEM((count, width), BF16),
             pltpu.VMEM((count, width), F32),
             pltpu.VMEM((heads, 256, 128), BF16),
-            pltpu.VMEM((4, len(LEVELS), HALF, HALF), BF16),
-            pltpu.VMEM((4, HALF, HALF), BF16),
+            pltpu.VMEM((2 * heads, len(LEVELS), HALF, HALF), BF16),
+            pltpu.VMEM((2 * heads, HALF, HALF), BF16),
             pltpu.VMEM((PLANE, 256, 128), BF16),
             pltpu.VMEM((PLANE, 256, 128), BF16),
             pltpu.VMEM((256, 128), BF16),
@@ -714,7 +827,7 @@
             pltpu.VMEM((3, rows, model), BF16),
             pltpu.VMEM((2, rows, model), F32),
             pltpu.VMEM((3, rows, model), BF16),
-            dma((9,)), dma((6,)), dma((6,)), dma((3,)), dma((3,)), dma((PLANE,)), dma((heads,)),
+            dma((15,)), dma((6,)), dma((6,)), dma((3,)), dma((3,)), dma((PLANE,)), dma((heads,)),
             dma((heads,)), dma((PLANE,)), dma((GROUP,)), dma((GROUP,)),
             dma((PLANE,)), dma((heads,)), dma((6,)), dma((6,)),
         ],

time: 61.2 us -> 56.2 us (0.918)
  Pallas kernels: 59.1 us -> 55.4 us
  local copies, waits for them, and re-layouts: 1.69 us -> 0.72 us
    pallas_call x1, Pallas kernels: 59.1 us -> 55.4 us  [layer(): pl.pallas_call(functools.partial(kernel, depth), name='layer', out_shape=...]
    unnamed x1, local copies, waits for them, and re-layouts: 1.69 us -> 0.72 us
where the time goes in v5:
time: 56.2 us; the launch traced here: 56.1 us
  Pallas kernels  55.4 us (99%)
  local copies, waits for them, and re-layouts  0.72 us (1%)
    pallas_call x1, Pallas kernels, layer(): pl.pallas_call(functools.partial(kernel, depth), name='layer', out_shape=...  55.4 us

profile of v5, /device:TPU:192, one launch (start us, length us, event | category | flops | bytes accessed | tf_op | source)
XLA Modules:
  0.0 56.1 jit_solution(3365568446818768961)
XLA Ops:
  0.0 55.4 %layer.1 = bf16[64,2304]{1,0:T(8,128)(2,1)S(1)} custom-call(bf16[64,2304]{1,0:T(8,128)(2,1)} %x_hbm.1, bf16[3,2304,512]{2,1,0:T(8,128)(2,1)} %bitcast.4, bf16[2304,128]{1,0:T(8,128)(2,1)} %down_hbm.1, bf16[2304,128]{1,0:T(8,128)(2,1)} %gdown_hbm.1, bf16[4,2304]{1,0:T(4,128)(2,1)} %bitcast.5, bf16[128,512]{1,0:T(8,128)(2,1)} %up_hbm.1, ...), custom_call_target="tpu_custom_call" | custom-call | tf_op jit(solution)/shard_map/layer/pallas_call | solution.py:784
  55.4 0.7 %copy.15 = bf16[64,2304]{1,0:T(8,128)(2,1)} copy(bf16[64,2304]{1,0:T(8,128)(2,1)S(1)} %layer.1) | data formatting | bytes 589824

commit v6 on v5

--- a/solution.py
+++ b/solution.py
@@ -203,18 +203,8 @@
                 act(copy)
 
     each_edge(3, lambda copy: copy.start())
-    moves[0].wait_recv()
-    moves[2].wait_send()
-    moves[4].start()
-    moves[1].wait_recv()
-    moves[3].wait_send()
-    moves[5].start()
-    each_edge(2, lambda copy: copy.start())
     for load in loads[1:14]:
         load.wait()
-    moves[2].wait_recv()
-    each_edge(0, lambda copy: copy.start())
-    moves[3].wait_recv()
 
     rate = jnp.concatenate(
         [jnp.exp(jnp.full((1, 128), dlog_ref[i], F32)) for i in range(heads)], axis=1
@@ -250,16 +240,25 @@
         if tail:
             proj_ref[c, HALO - EDGE : HALO, :] = got[size : size + EDGE]
 
-    near = (h, left, right)
-    project(0, near)
+    project(0, (h,))
     for c in range(3):
-        project_qkv(c, 0, near, 0)
-    moves[4].wait_recv()
-    moves[5].wait_recv()
-
-    @pl.when(s > 0)
-    def _():
-        edges[0][0].wait_recv()
+        project_qkv(c, 0, (h,), 0)
+
+    moves[0].wait_recv()
+    moves[2].wait_send()
+    moves[4].start()
+    moves[1].wait_recv()
+    moves[3].wait_send()
+    moves[5].start()
+    each_edge(2, lambda copy: copy.start())
+    moves[2].wait_recv()
+    each_edge(0, lambda copy: copy.start())
+    moves[3].wait_recv()
+
+    near = (left, right)
+    project(rows, near)
+    for c in range(3):
+        project_qkv(c, rows, near, 0)
 
     def decays(c):
         piece_of = fade_ref[c * HALF : (c + 1) * HALF, :]
@@ -271,15 +270,16 @@
             )
         )
 
-    def convolve(c):
+    def convolve(c, first, size):
         target = (q_ref, k_ref, v_ref)[c]
         taps = conv_ref[c].astype(F32)
-        mixed = proj_ref[c, pl.ds(HALO - 3, count), :] * taps[0:1]
+        at = HALO - 3 + first
+        mixed = proj_ref[c, pl.ds(at, size), :] * taps[0:1]
         for i in range(1, 4):
-            mixed = mixed + proj_ref[c, pl.ds(HALO - 3 + i, count), :] * taps[i : i + 1]
+            mixed = mixed + proj_ref[c, pl.ds(at + i, size), :] * taps[i : i + 1]
         mixed = (mixed * sigmoid(mixed)).astype(BF16).astype(F32)
         if c == 2:
-            target[...] = mixed
+            target[first : first + size, :] = mixed
             return
         for i in range(heads):
             lanes = slice(i * 128, (i + 1) * 128)
@@ -287,17 +287,39 @@
             scale = lax.rsqrt(jnp.sum(u * u, axis=1, keepdims=True) + 1e-06)
             if c == 0:
                 scale = scale * (128**-0.5)
-            target[:, lanes] = u * scale
-
-    project(3 * rows, (far,))
-    project_qkv(1, 3 * rows, (far,), HALO)
-    decays(0)
-    project_qkv(0, 3 * rows, (far,), HALO)
-    convolve(1)
-    decays(1)
-    project_qkv(2, 3 * rows, (far,), HALO)
-    convolve(0)
-    convolve(2)
+            target[first : first + size, lanes] = u * scale
+
+    far_square = lax.div(far, 2)
+    for c in range(2):
+
+        @pl.when(far_square == 1 - c)
+        def _():
+            decays(c)
+            for n in range(3):
+                convolve(n, c * HALF + EDGE, HALF - EDGE)
+
+    moves[4].wait_recv()
+    moves[5].wait_recv()
+
+    @pl.when(s > 0)
+    def _():
+        edges[0][0].wait_recv()
+
+    for c in range(2):
+
+        @pl.when(far_square == c)
+        def _():
+            project(3 * rows, (far,))
+            project_qkv(1, 3 * rows, (far,), HALO)
+            decays(c)
+            project_qkv(0, 3 * rows, (far,), HALO)
+            convolve(1, c * HALF, HALF)
+            project_qkv(2, 3 * rows, (far,), HALO)
+            convolve(0, c * HALF, HALF)
+            convolve(2, c * HALF, HALF)
+            for n in range(3):
+                convolve(n, (1 - c) * HALF, EDGE)
+
     beta = strength_ref[...]
 
     t = lax.broadcasted_iota(jnp.int32, (HALF, HALF), 0)

time: 56.2 us -> 56 us (level)
  no operation moved by 1% of the time
where the time goes in v6:
time: 56 us; the launch traced here: 55.9 us
  Pallas kernels  55.2 us (99%)
  local copies, waits for them, and re-layouts  0.72 us (1%)
    pallas_call x1, Pallas kernels, layer(): pl.pallas_call(functools.partial(kernel, depth), name='layer', out_shape=...  55.2 us

profile of v6, /device:TPU:192, one launch (start us, length us, event | category | flops | bytes accessed | tf_op | source)
XLA Modules:
  0.0 55.9 jit_solution(15355569413129360361)
XLA Ops:
  0.0 55.2 %layer.1 = bf16[64,2304]{1,0:T(8,128)(2,1)S(1)} custom-call(bf16[64,2304]{1,0:T(8,128)(2,1)} %x_hbm.1, bf16[3,2304,512]{2,1,0:T(8,128)(2,1)} %bitcast.4, bf16[2304,128]{1,0:T(8,128)(2,1)} %down_hbm.1, bf16[2304,128]{1,0:T(8,128)(2,1)} %gdown_hbm.1, bf16[4,2304]{1,0:T(4,128)(2,1)} %bitcast.5, bf16[128,512]{1,0:T(8,128)(2,1)} %up_hbm.1, ...), custom_call_target="tpu_custom_call" | custom-call | tf_op jit(solution)/shard_map/layer/pallas_call | solution.py:806
  55.2 0.7 %copy.15 = bf16[64,2304]{1,0:T(8,128)(2,1)} copy(bf16[64,2304]{1,0:T(8,128)(2,1)S(1)} %layer.1) | data formatting | bytes 589824

commit v7 on v5

--- a/solution.py
+++ b/solution.py
@@ -51,7 +51,7 @@
     x_ref, w_ref, dg_ref, beta_ref, up_ref, gup_ref, conv_ref, dlog_ref, bias_ref, span_ref,
     gain_ref, ow_ref,
     proj_ref, fade_ref, strength_ref, q_ref, k_ref, v_ref, e_ref, o_ref, r_ref, gate_ref, z_ref,
-    mix_ref, attend_ref, zin, pre, total, zall, chain, link, held, entry, lead, state, normed, part, sums, inbox,
+    mix_ref, faded_ref, attend_ref, zin, pre, total, zall, chain, link, held, entry, lead, state, normed, part, sums, inbox,
     l_sem, x_send, x_recv, e_sem, f_sem, g_send, g_recv,
     a_send, a_recv, b_send, b_recv, c_send, c_recv, d_send, d_recv,
 ):
@@ -106,7 +106,7 @@
 
         @pl.when(group == 1)
         def _():
-            feeder = jnp.where(rank < 2, GROUP - 1, 0)
+            feeder = jnp.where(rank < GROUP - 1, GROUP - 1, 0)
             pl.semaphore_signal(
                 barrier, 1, device_id={"seq": feeder * PLANE + p}, device_id_type=MESH
             )
@@ -114,7 +114,7 @@
     greeted = (
         2
         + jnp.where(owner, PLANE - 1 + GROUP - 1, PLANE // 2 + 1)
-        + jnp.where(jnp.logical_and(owner, feeds), 2, 0)
+        + jnp.where(jnp.logical_and(owner, feeds), jnp.where(rank == 0, 1, GROUP - 1), 0)
         + jnp.where(has_next, jnp.where(h == 2, 2, jnp.where(h == 1, 0, 1)), 0)
     )
 
@@ -203,18 +203,8 @@
                 act(copy)
 
     each_edge(3, lambda copy: copy.start())
-    moves[0].wait_recv()
-    moves[2].wait_send()
-    moves[4].start()
-    moves[1].wait_recv()
-    moves[3].wait_send()
-    moves[5].start()
-    each_edge(2, lambda copy: copy.start())
     for load in loads[1:14]:
         load.wait()
-    moves[2].wait_recv()
-    each_edge(0, lambda copy: copy.start())
-    moves[3].wait_recv()
 
     rate = jnp.concatenate(
         [jnp.exp(jnp.full((1, 128), dlog_ref[i], F32)) for i in range(heads)], axis=1
@@ -250,19 +240,8 @@
         if tail:
             proj_ref[c, HALO - EDGE : HALO, :] = got[size : size + EDGE]
 
-    near = (h, left, right)
-    project(0, near)
-    for c in range(3):
-        project_qkv(c, 0, near, 0)
-    moves[4].wait_recv()
-    moves[5].wait_recv()
-
-    @pl.when(s > 0)
-    def _():
-        edges[0][0].wait_recv()
-
     def decays(c):
-        piece_of = fade_ref[c * HALF : (c + 1) * HALF, :]
+        piece_of = fade_ref[pl.ds(pl.multiple_of(c * HALF, HALF), HALF), :]
         top = piece_of.astype(BF16)
         rest = (piece_of - top.astype(F32)).astype(BF16)
         e_ref[c] = jnp.exp(
@@ -270,6 +249,34 @@
                 span_ref[...], jnp.concatenate([top, rest], axis=0), preferred_element_type=F32
             )
         )
+
+    project(0, (h,))
+    for c in range(3):
+        project_qkv(c, 0, (h,), 0)
+
+    moves[0].wait_recv()
+    moves[2].wait_send()
+    moves[4].start()
+    moves[1].wait_recv()
+    moves[3].wait_send()
+    moves[5].start()
+    each_edge(2, lambda copy: copy.start())
+    moves[2].wait_recv()
+    each_edge(0, lambda copy: copy.start())
+    moves[3].wait_recv()
+
+    near = (left, right)
+    project(rows, near)
+    for c in range(3):
+        project_qkv(c, rows, near, 0)
+    far_square = lax.div(far, 2)
+    decays(1 - far_square)
+    moves[4].wait_recv()
+    moves[5].wait_recv()
+
+    @pl.when(s > 0)
+    def _():
+        edges[0][0].wait_recv()
 
     def convolve(c):
         target = (q_ref, k_ref, v_ref)[c]
@@ -291,10 +298,9 @@
 
     project(3 * rows, (far,))
     project_qkv(1, 3 * rows, (far,), HALO)
-    decays(0)
+    decays(far_square)
     project_qkv(0, 3 * rows, (far,), HALO)
     convolve(1)
-    decays(1)
     project_qkv(2, 3 * rows, (far,), HALO)
     convolve(0)
     convolve(2)
@@ -326,31 +332,35 @@
     def unit_of(i, c):
         return 2 * i + c
 
-    def mix(i, c, n, attend):
-        kc, qc = k_ref[rows_of[c], lanes_of[i]], q_ref[rows_of[c], lanes_of[i]]
+    def mix(i, c, n):
+        kc = k_ref[rows_of[c], lanes_of[i]]
         if n == 0:
             strength[i, c] = jnp.broadcast_to(beta[rows_of[c], i : i + 1], (HALF, 128))
-            own = jnp.sum(qc * kc, axis=1, keepdims=True) * strength[i, c]
-            attend = jnp.where(diagonal, own, 0.0)
-        size = LEVELS[n]
         fade = e_ref[c, n * HALF : (n + 1) * HALF, lanes_of[i]]
-        late = (row & size) != 0
+        late = (row & LEVELS[n]) != 0
         kx = (kc * fade * jnp.where(late, 1.0, strength[i, c])).astype(BF16)
-        qx = (qc * fade).astype(BF16)
-        both = mm(jnp.concatenate([kx, qx], axis=0), kx, ((1,), (1,)))
-        mix_ref[unit_of(i, c), n] = jnp.where(masks[n], both[:HALF], 0.0).astype(BF16)
-        attend = jnp.where(masks[n], both[HALF:], attend)
-        if n == len(LEVELS) - 1:
-            attend_ref[unit_of(i, c)] = attend.astype(BF16)
-        return attend
+        faded_ref[unit_of(i, c), n] = kx
+        mix_ref[unit_of(i, c), n] = jnp.where(masks[n], mm(kx, kx, ((1,), (1,))), 0.0).astype(BF16)
 
     def mixes(some):
         for i in some:
             for c in range(2):
-                attend = None
                 for n in range(len(LEVELS)):
-                    attend = mix(i, c, n, attend)
+                    mix(i, c, n)
                     yield
+
+    def attends(some):
+        for i in some:
+            for c in range(2):
+                kc, qc = k_ref[rows_of[c], lanes_of[i]], q_ref[rows_of[c], lanes_of[i]]
+                own = jnp.sum(qc * kc, axis=1, keepdims=True) * strength[i, c]
+                attend = jnp.where(diagonal, own, 0.0)
+                for n in range(len(LEVELS)):
+                    qx = qc * e_ref[c, n * HALF : (n + 1) * HALF, lanes_of[i]]
+                    both = mm(qx, faded_ref[unit_of(i, c), n], ((1,), (1,)))
+                    attend = jnp.where(masks[n], both, attend)
+                attend_ref[unit_of(i, c)] = attend.astype(BF16)
+                yield
 
     def doublings(some):
         units = [(i, c) for i in some for c in range(2)]
@@ -377,15 +387,12 @@
         fall = {u: e_ref[u[1], (n + 1) * HALF : (n + 2) * HALF, lanes_of[u[0]]] for u in units}
         whole = {u: rise[u][HALF - 1 : HALF] for u in units}
         k_rise = {u: k_ref[rows_of[u[1]], lanes_of[u[0]]] * rise[u] for u in units}
-        q_rise = {u: q_ref[rows_of[u[1]], lanes_of[u[0]]] * rise[u] for u in units}
         k_fall = {
             u: k_ref[rows_of[u[1]], lanes_of[u[0]]] * fall[u] * strength[u] for u in units
         }
         cross, first, second = {}, {}, {}
         for i in some:
-            cross[i] = mm(
-                jnp.concatenate([k_rise[i, 1], q_rise[i, 1]], axis=0), k_fall[i, 0], ((1,), (1,))
-            ).astype(BF16)
+            cross[i] = mm(k_rise[i, 1], k_fall[i, 0], ((1,), (1,))).astype(BF16)
         for i in some:
             first[i] = mm(
                 inverse[i, 0],
@@ -398,7 +405,7 @@
             start = jnp.concatenate(
                 [v_ref[rows_of[1], lanes_of[i]], k_rise[i, 1] * whole[i, 0]], axis=1
             )
-            second[i] = mm(inverse[i, 1], start - late_part[i][:HALF]).astype(BF16)
+            second[i] = mm(inverse[i, 1], start - late_part[i]).astype(BF16)
         yield
         for i in some:
             stop = jnp.concatenate(
@@ -408,15 +415,19 @@
             move = jnp.where(diagonal, whole[i, 0] * whole[i, 1], 0.0) - maps[128:]
             z_ref[i, 0:128] = move.astype(BF16)
             z_ref[i, 128:256] = maps[:128].astype(BF16)
-            parts[i] = (q_rise, whole, first, second, late_part)
+            parts[i] = (rise, whole, first, second, k_fall)
 
     def outputs_of(some):
         for i in some:
-            q_rise, whole, first, second, late_part = parts[i]
+            rise, whole, first, second, k_fall = parts[i]
             lanes = lanes_of[i]
+            q_rise = {
+                (i, c): q_ref[rows_of[c], lanes] * rise[i, c] for c in range(2)
+            }
+            cross = mm(q_rise[i, 1], k_fall[i, 0], ((1,), (1,)))
             out = [
                 mm(attend_ref[unit_of(i, 0)], first[i]),
-                late_part[i][HALF:] + mm(attend_ref[unit_of(i, 1)], second[i]),
+                mm(cross, first[i]) + mm(attend_ref[unit_of(i, 1)], second[i]),
             ]
             for c in range(2):
                 o_ref[rows_of[c], lanes] = out[c][:, :128]
@@ -451,11 +462,10 @@
     other = doublings(late_heads)
     together(maps_of(early), other, 1)
     send_maps(early)
-    outputs = outputs_of(early)
-    together(other, outputs, 1)
-    finish(outputs, maps_of(late_heads))
+    finish(other, maps_of(late_heads))
     send_maps(late_heads)
-    finish(outputs_of(late_heads))
+    for some in (early, late_heads):
+        finish(attends(some), outputs_of(some))
 
     def to_group(k, at):
         return pltpu.make_async_remote_copy(
@@ -478,15 +488,25 @@
         )
 
     def to_next(k):
-        target = jnp.where(rank == 0, 2 * GROUP - 1 - k, GROUP + k)
+        target = jnp.where(rank == 0, 2 * GROUP - 1, 2 * GROUP - 2 - k)
         return pltpu.make_async_remote_copy(
             src_ref=chain,
             dst_ref=held,
             send_sem=f_sem.at[k],
-            recv_sem=f_sem.at[2],
+            recv_sem=f_sem.at[3],
             device_id={"seq": target * PLANE + p},
             device_id_type=MESH,
         )
+
+    def feed(act):
+        @pl.when(feeds)
+        def _():
+            act(to_next(0))
+
+        @pl.when(jnp.logical_and(feeds, rank > 0))
+        def _():
+            for k in range(1, GROUP - 1):
+                act(to_next(k))
 
     def prefix_to(q):
         return pltpu.make_async_remote_copy(
@@ -609,10 +629,7 @@
                     else:
                         chain[...] = moved(chain[...], zall[k])
 
-            @pl.when(feeds)
-            def _():
-                for k in range(2):
-                    to_next(k).start()
+            feed(lambda copy: copy.start())
 
         @pl.when(group == 1)
         def _():
@@ -752,10 +769,7 @@
     def _():
         group_copies(lambda copy: copy.wait_send())
 
-        @pl.when(feeds)
-        def _():
-            for k in range(2):
-                to_next(k).wait_send()
+        feed(lambda copy: copy.wait_send())
 
         for d in FAR_FIRST:
             q = lax.rem(p + d, PLANE)
@@ -812,6 +826,7 @@
             pltpu.VMEM((count, width), F32),
             pltpu.VMEM((heads, 256, 128), BF16),
             pltpu.VMEM((2 * heads, len(LEVELS), HALF, HALF), BF16),
+            pltpu.VMEM((2 * heads, len(LEVELS), HALF, 128), BF16),
             pltpu.VMEM((2 * heads, HALF, HALF), BF16),
             pltpu.VMEM((PLANE, 256, 128), BF16),
             pltpu.VMEM((PLANE, 256, 128), BF16),
@@ -827,7 +842,7 @@
             pltpu.VMEM((3, rows, model), BF16),
             pltpu.VMEM((2, rows, model), F32),
             pltpu.VMEM((3, rows, model), BF16),
-            dma((15,)), dma((6,)), dma((6,)), dma((3,)), dma((3,)), dma((PLANE,)), dma((heads,)),
+            dma((15,)), dma((6,)), dma((6,)), dma((3,)), dma((4,)), dma((PLANE,)), dma((heads,)),
             dma((heads,)), dma((PLANE,)), dma((GROUP,)), dma((GROUP,)),
             dma((PLANE,)), dma((heads,)), dma((6,)), dma((6,)),
         ],

time: 56.2 us -> 54.4 us (0.968)
  Pallas kernels: 55.4 us -> 53.6 us
    pallas_call x1, Pallas kernels: 55.4 us -> 53.6 us  [layer(): pl.pallas_call(functools.partial(kernel, depth), name='layer', out_shape=...]
where the time goes in v7:
time: 54.4 us; the launch traced here: 54.3 us
  Pallas kernels  53.6 us (99%)
  local copies, waits for them, and re-layouts  0.72 us (1%)
    pallas_call x1, Pallas kernels, layer(): pl.pallas_call(functools.partial(kernel, depth), name='layer', out_shape=...  53.6 us

profile of v7, /device:TPU:192, one launch (start us, length us, event | category | flops | bytes accessed | tf_op | source)
XLA Modules:
  0.0 54.3 jit_solution(11730443606617022795)
XLA Ops:
  0.0 53.6 %layer.1 = bf16[64,2304]{1,0:T(8,128)(2,1)S(1)} custom-call(bf16[64,2304]{1,0:T(8,128)(2,1)} %x_hbm.1, bf16[3,2304,512]{2,1,0:T(8,128)(2,1)} %bitcast.4, bf16[2304,128]{1,0:T(8,128)(2,1)} %down_hbm.1, bf16[2304,128]{1,0:T(8,128)(2,1)} %gdown_hbm.1, bf16[4,2304]{1,0:T(4,128)(2,1)} %bitcast.5, bf16[128,512]{1,0:T(8,128)(2,1)} %up_hbm.1, ...), custom_call_target="tpu_custom_call" | custom-call | tf_op jit(solution)/shard_map/layer/pallas_call | solution.py:798
  53.6 0.7 %copy.15 = bf16[64,2304]{1,0:T(8,128)(2,1)} copy(bf16[64,2304]{1,0:T(8,128)(2,1)S(1)} %layer.1) | data formatting | bytes 589824

commit v8 on v7

--- a/solution.py
+++ b/solution.py
@@ -19,7 +19,7 @@
 PLANE = 8
 GROUP = 4
 FAR_FIRST = (4, 5, 2, 3, 6, 7, 1)
-ENTRIES = (7, 4, 2, 3, 6, 1)
+ENTRIES = (7, 4, 6, 2, 1, 3)
 
 
 def span_matrix():
@@ -327,7 +327,7 @@
             device_id_type=MESH,
         )
 
-    strength, inverse = {}, {}
+    strength, written, inverse = {}, {}, {}
 
     def unit_of(i, c):
         return 2 * i + c
@@ -336,9 +336,20 @@
         kc = k_ref[rows_of[c], lanes_of[i]]
         if n == 0:
             strength[i, c] = jnp.broadcast_to(beta[rows_of[c], i : i + 1], (HALF, 128))
+            written[i, c] = kc * strength[i, c]
         fade = e_ref[c, n * HALF : (n + 1) * HALF, lanes_of[i]]
-        late = (row & LEVELS[n]) != 0
-        kx = (kc * fade * jnp.where(late, 1.0, strength[i, c])).astype(BF16)
+        size = LEVELS[n]
+        if size < 8:
+            chosen = jnp.where((row & size) != 0, kc, written[i, c])
+        else:
+            chosen = jnp.concatenate(
+                [
+                    (kc if at & size else written[i, c])[at : at + size]
+                    for at in range(0, HALF, size)
+                ],
+                axis=0,
+            )
+        kx = (chosen * fade).astype(BF16)
         faded_ref[unit_of(i, c), n] = kx
         mix_ref[unit_of(i, c), n] = jnp.where(masks[n], mm(kx, kx, ((1,), (1,))), 0.0).astype(BF16)
 
@@ -388,7 +399,7 @@
         whole = {u: rise[u][HALF - 1 : HALF] for u in units}
         k_rise = {u: k_ref[rows_of[u[1]], lanes_of[u[0]]] * rise[u] for u in units}
         k_fall = {
-            u: k_ref[rows_of[u[1]], lanes_of[u[0]]] * fall[u] * strength[u] for u in units
+            u: written[u] * fall[u] for u in units
         }
         cross, first, second = {}, {}, {}
         for i in some:
@@ -551,7 +562,7 @@
         return (mm(state_in, both[0:128]) + both[128:256].astype(F32)).astype(BF16)
 
     def group_copies(act):
-        for k in range(GROUP):
+        for k in (3, 0, 2, 1):
             @pl.when(jnp.logical_and(jnp.logical_and(group == 0, rank == 0), k > 0))
             def _():
                 act(to_group(k, shift_only))
@@ -688,7 +699,7 @@
         device_id={"seq": base + lax.rem(p + PLANE - 2, PLANE)},
         device_id_type=MESH,
     )
-    for d in (1, 0, 3, 2):
+    for d in (0, 1, 3, 2):
         i = lax.rem(y + d, heads)
 
         @pl.when(jnp.logical_and(p != 2 * i, z > 0))

time: 54.4 us -> 54.3 us (level)
  Pallas kernels: 53.6 us -> 53 us
    pallas_call x1, Pallas kernels: 53.6 us -> 53 us  [layer(): pl.pallas_call(functools.partial(kernel, depth), name='layer', out_shape=...]
where the time goes in v8:
time: 54.3 us; the launch traced here: 53.7 us
  Pallas kernels  53 us (98%)
  local copies, waits for them, and re-layouts  0.72 us (1%)
    pallas_call x1, Pallas kernels, layer(): pl.pallas_call(functools.partial(kernel, depth), name='layer', out_shape=...  53 us

profile of v8, /device:TPU:192, one launch (start us, length us, event | category | flops | bytes accessed | tf_op | source)
XLA Modules:
  0.0 53.7 jit_solution(1338837020116150144)
XLA Ops:
  0.0 53.0 %layer.1 = bf16[64,2304]{1,0:T(8,128)(2,1)S(1)} custom-call(bf16[64,2304]{1,0:T(8,128)(2,1)} %x_hbm.1, bf16[3,2304,512]{2,1,0:T(8,128)(2,1)} %bitcast.4, bf16[2304,128]{1,0:T(8,128)(2,1)} %down_hbm.1, bf16[2304,128]{1,0:T(8,128)(2,1)} %gdown_hbm.1, bf16[4,2304]{1,0:T(4,128)(2,1)} %bitcast.5, bf16[128,512]{1,0:T(8,128)(2,1)} %up_hbm.1, ...), custom_call_target="tpu_custom_call" | custom-call | tf_op jit(solution)/shard_map/layer/pallas_call | solution.py:809
  53.0 0.7 %copy.15 = bf16[64,2304]{1,0:T(8,128)(2,1)} copy(bf16[64,2304]{1,0:T(8,128)(2,1)S(1)} %layer.1) | data formatting | bytes 589824

commit v9 on v8

--- a/solution.py
+++ b/solution.py
@@ -299,10 +299,8 @@
     project(3 * rows, (far,))
     project_qkv(1, 3 * rows, (far,), HALO)
     decays(far_square)
-    project_qkv(0, 3 * rows, (far,), HALO)
     convolve(1)
     project_qkv(2, 3 * rows, (far,), HALO)
-    convolve(0)
     convolve(2)
     beta = strength_ref[...]
 
@@ -475,6 +473,8 @@
     send_maps(early)
     finish(other, maps_of(late_heads))
     send_maps(late_heads)
+    project_qkv(0, 3 * rows, (far,), HALO)
+    convolve(0)
     for some in (early, late_heads):
         finish(attends(some), outputs_of(some))
 
@@ -719,9 +719,9 @@
     loads[14].wait()
 
 
-    def partial(to):
+    def partial(to, lanes=slice(None)):
         at = pl.ds(pl.multiple_of(to * rows, 16), rows)
-        return jnp.dot(normed[at, :], ow_ref[...], preferred_element_type=F32)
+        return jnp.dot(normed[at, :], ow_ref[:, lanes], preferred_element_type=F32)
 
     def pass_on(k, src, dst, target):
         return pltpu.make_async_remote_copy(
@@ -734,26 +734,37 @@
         )
 
     top, low = pl.ds(0, half), pl.ds(half, half)
-    part[0] = partial(far).astype(BF16)
-    far_right = pass_on(0, part.at[0, top], inbox.at[0, top], right)
-    far_left = pass_on(1, part.at[0, low], inbox.at[0, low], left)
-    far_right.start()
-    far_left.start()
+    columns = out_ref.shape[1]
+    split = columns // 2 // 128 * 128
+    far_right, far_left = [], []
+    for n, (first_lane, end_lane) in enumerate([(0, split), (split, columns)]):
+        part[0, :, first_lane:end_lane] = partial(far, slice(first_lane, end_lane)).astype(BF16)
+        some = pl.ds(first_lane, end_lane - first_lane)
+        far_right.append(
+            pass_on(2 * n, part.at[0, top, some], inbox.at[0, top, some], right)
+        )
+        far_left.append(
+            pass_on(2 * n + 1, part.at[0, low, some], inbox.at[0, low, some], left)
+        )
+        far_right[n].start()
+        far_left[n].start()
     sums[0] = partial(right)
     part[1, low] = sums[0, low].astype(BF16)
-    right_low = pass_on(2, part.at[1, low], inbox.at[1, low], right)
+    right_low = pass_on(4, part.at[1, low], inbox.at[1, low], right)
     right_low.start()
     sums[1] = partial(left)
     part[2, top] = sums[1, top].astype(BF16)
-    left_top = pass_on(3, part.at[2, top], inbox.at[2, top], left)
+    left_top = pass_on(5, part.at[2, top], inbox.at[2, top], left)
     left_top.start()
-    far_right.wait_recv()
+    for copy in far_right:
+        copy.wait_recv()
     part[1, top] = (sums[0, top] + inbox[0, top].astype(F32)).astype(BF16)
-    right_top = pass_on(4, part.at[1, top], inbox.at[1, top], right)
+    right_top = pass_on(6, part.at[1, top], inbox.at[1, top], right)
     right_top.start()
-    far_left.wait_recv()
+    for copy in far_left:
+        copy.wait_recv()
     part[2, low] = (sums[1, low] + inbox[0, low].astype(F32)).astype(BF16)
-    left_low = pass_on(5, part.at[2, low], inbox.at[2, low], left)
+    left_low = pass_on(7, part.at[2, low], inbox.at[2, low], left)
     left_low.start()
     own = partial(h)
     right_low.wait_recv()
@@ -762,7 +773,7 @@
     left_low.wait_recv()
     out_ref[...] = (own + inbox[1].astype(F32) + inbox[2].astype(F32)).astype(BF16)
 
-    for copy in (far_right, far_left, right_low, left_top, right_top, left_low):
+    for copy in (*far_right, *far_left, right_low, left_top, right_top, left_low):
         copy.wait_send()
     for n in (0, 1, 4, 5):
         moves[n].wait_send()
@@ -855,7 +866,7 @@
             pltpu.VMEM((3, rows, model), BF16),
             dma((15,)), dma((6,)), dma((6,)), dma((3,)), dma((4,)), dma((PLANE,)), dma((heads,)),
             dma((heads,)), dma((PLANE,)), dma((GROUP,)), dma((GROUP,)),
-            dma((PLANE,)), dma((heads,)), dma((6,)), dma((6,)),
+            dma((PLANE,)), dma((heads,)), dma((8,)), dma((8,)),
         ],
         compiler_params=pltpu.CompilerParams(
             collective_id=0, has_side_effects=True, vmem_limit_bytes=56 << 20

time: 54.3 us -> 53.8 us (level)
  no operation moved by 1% of the time
where the time goes in v9:
time: 53.8 us; the launch traced here: 53.2 us
  Pallas kernels  52.5 us (98%)
  local copies, waits for them, and re-layouts  0.72 us (1%)
    pallas_call x1, Pallas kernels, layer(): pl.pallas_call(functools.partial(kernel, depth), name='layer', out_shape=...  52.5 us

profile of v9, /device:TPU:192, one launch (start us, length us, event | category | flops | bytes accessed | tf_op | source)
XLA Modules:
  0.0 53.2 jit_solution(8507715909505662685)
XLA Ops:
  0.0 52.5 %layer.1 = bf16[64,2304]{1,0:T(8,128)(2,1)S(1)} custom-call(bf16[64,2304]{1,0:T(8,128)(2,1)} %x_hbm.1, bf16[3,2304,512]{2,1,0:T(8,128)(2,1)} %bitcast.4, bf16[2304,128]{1,0:T(8,128)(2,1)} %down_hbm.1, bf16[2304,128]{1,0:T(8,128)(2,1)} %gdown_hbm.1, bf16[4,2304]{1,0:T(4,128)(2,1)} %bitcast.5, bf16[128,512]{1,0:T(8,128)(2,1)} %up_hbm.1, ...), custom_call_target="tpu_custom_call" | custom-call | tf_op jit(solution)/shard_map/layer/pallas_call | solution.py:820
  52.5 0.7 %copy.15 = bf16[64,2304]{1,0:T(8,128)(2,1)} copy(bf16[64,2304]{1,0:T(8,128)(2,1)S(1)} %layer.1) | data formatting | bytes 589824

commit v10 on v9

--- a/solution.py
+++ b/solution.py
@@ -465,10 +465,14 @@
 
     early, late_heads = range(0, heads, 2), range(1, heads, 2)
     finish(mixes(early))
-    other = mixes(late_heads)
-    together(doublings(early), other, 3)
-    finish(other)
-    other = doublings(late_heads)
+    mixing, other = mixes(late_heads), doublings(late_heads)
+    for step, _ in enumerate(doublings(early)):
+        if step < 6:
+            for _ in range(5):
+                next(mixing, None)
+        else:
+            finish(mixing)
+            next(other)
     together(maps_of(early), other, 1)
     send_maps(early)
     finish(other, maps_of(late_heads))

time: 53.8 us -> 53.5 us (level)
  Pallas kernels: 52.5 us -> 51.8 us
    pallas_call x1, Pallas kernels: 52.5 us -> 51.8 us  [layer(): pl.pallas_call(functools.partial(kernel, depth), name='layer', out_shape=...]
where the time goes in v10:
time: 53.5 us; the launch traced here: 52.6 us
  Pallas kernels  51.8 us (97%)
  local copies, waits for them, and re-layouts  0.72 us (1%)
    pallas_call x1, Pallas kernels, layer(): pl.pallas_call(functools.partial(kernel, depth), name='layer', out_shape=...  51.8 us

profile of v10, /device:TPU:192, one launch (start us, length us, event | category | flops | bytes accessed | tf_op | source)
XLA Modules:
  0.0 52.6 jit_solution(15179049594559749115)
XLA Ops:
  0.0 51.8 %layer.1 = bf16[64,2304]{1,0:T(8,128)(2,1)S(1)} custom-call(bf16[64,2304]{1,0:T(8,128)(2,1)} %x_hbm.1, bf16[3,2304,512]{2,1,0:T(8,128)(2,1)} %bitcast.4, bf16[2304,128]{1,0:T(8,128)(2,1)} %down_hbm.1, bf16[2304,128]{1,0:T(8,128)(2,1)} %gdown_hbm.1, bf16[4,2304]{1,0:T(4,128)(2,1)} %bitcast.5, bf16[128,512]{1,0:T(8,128)(2,1)} %up_hbm.1, ...), custom_call_target="tpu_custom_call" | custom-call | tf_op jit(solution)/shard_map/layer/pallas_call | solution.py:824
  51.8 0.7 %copy.15 = bf16[64,2304]{1,0:T(8,128)(2,1)} copy(bf16[64,2304]{1,0:T(8,128)(2,1)S(1)} %layer.1) | data formatting | bytes 589824
